TPU v7x, 32 devices: a whole 2x2x4 slice. The times are simulated.
32 devices in a mesh: groups: 2 (over y), seq: 4 (over z), head: 2 (over x), rep: 2 (over core).
Axes of the slice: x: 2, y: 2, z: 4, core: 2. Of those that a mesh axis runs over, the one named last changes fastest.
Arguments:
- queries: bfloat16 [32768, 16, 128], P(('groups', 'seq'), ('head', 'rep')), parts along dimension 0, may hold values from -8 to 8
- keys: bfloat16 [32768, 128], P(('groups', 'seq')), parts along dimension 0, may hold values from -6 to 6
- values: bfloat16 [32768, 128], P(('groups', 'seq')), parts along dimension 0, may hold values from -6 to 6
- query_maps: bfloat16 [32, 128, 128], P(('groups', 'head', 'rep')), parts along dimension 0, may hold values from -0.5 to 0.5
- key_map: bfloat16 [256, 128], P('groups'), parts along dimension 0, may hold values from -0.046875 to 0.046875
- linear_cotangent: bfloat16 [32768, 16, 128], P(('groups', 'seq'), ('head', 'rep')), parts along dimension 0, may hold values from -0.046875 to 0.046875
Outputs:
- softmax_out: bfloat16 [32768, 16, 128], P(('groups', 'seq'), ('head', 'rep')), parts along dimension 0
- linear_out: bfloat16 [32768, 16, 128], P(('groups', 'seq'), ('head', 'rep')), parts along dimension 0
- map_gradient: float32 [256, 16, 128], P(('groups', 'seq'), ('head', 'rep')), parts along dimension 0
There are 2 independent parts, one for each index of `groups`. A program takes and returns all parts, laid end to end along the dimension named above; each array names one. Nothing has to cross between parts.
All inputs are finite; a program needn't handle non-finite values.
Results may differ from a plain program's by a relative error of at most 0.0058.
Values may be sent and summed in bfloat16 or wider, within the bound.
A program may use at most 128 MiB of HBM per device.

v0:
```python
import functools

import jax
import jax.numpy as jnp
from jax import lax
from jax.experimental import pallas as pl
from jax.experimental.pallas import tpu as pltpu
from jax.sharding import PartitionSpec as P

W = 512
TILE = 128
MESH = pl.DeviceIdType.MESH


def nt(a, b):
    return lax.dot_general(a, b, (((1,), (1,)), ((), ())), preferred_element_type=jnp.float32)


def tn(a, b):
    return lax.dot_general(a, b, (((0,), (0,)), ((), ())), preferred_element_type=jnp.float32)


def nn(a, b):
    return jnp.dot(a, b, preferred_element_type=jnp.float32)


def head_masks(rows, heads, inner, hd):
    def mask(parts, of_head):
        shape = (rows, parts * hd)
        head = lax.broadcasted_iota(jnp.int32, shape, 0) % heads
        part = lax.broadcasted_iota(jnp.int32, shape, 1) // hd
        return jnp.where(of_head(head) == part, 1.0, 0.0).astype(jnp.bfloat16)

    return mask(heads // inner, lambda h: h // inner), mask(inner, lambda h: h % inner)


def ahead_of(rows, start, heads):
    shape = (rows, TILE)
    local = (lax.broadcasted_iota(jnp.int32, shape, 0) + start) // heads
    return local, lax.broadcasted_iota(jnp.int32, shape, 1) > local


def window_softmax(q, k_win, v_win, ahead, invalid=None):
    hd = q.shape[1]
    mids = W // TILE
    scale = hd ** (-0.5) * 1.4426950408889634
    scores = nt(q, k_win)
    parts = [scores[:, j * TILE : (j + 1) * TILE] for j in range(mids + 1)]
    if invalid is not None:
        parts = [p + invalid[j] if j < mids else p for j, p in enumerate(parts)]
    kept = [jnp.where(ahead, parts[0], parts[mids])] + parts[1:mids]
    highest = jnp.max(functools.reduce(jnp.maximum, kept), axis=1, keepdims=True)
    kept = [jnp.exp2((p - highest) * scale) for p in kept]
    weights = jnp.concatenate(
        [jnp.where(ahead, kept[0], 0.0).astype(jnp.bfloat16)]
        + [p.astype(jnp.bfloat16) for p in kept[1:]]
        + [jnp.where(ahead, 0.0, kept[0]).astype(jnp.bfloat16)], 1
    )
    soft = nn(weights, v_win)
    return (soft[:, :hd] / soft[:, hd:]).astype(jnp.bfloat16)


def seq_barrier(rank, count):
    barrier = pltpu.get_barrier_semaphore()
    for k in range(1, count):
        pl.semaphore_signal(
            barrier, inc=1, device_id={"seq": lax.rem(rank + k, count)}, device_id_type=MESH
        )
    return barrier


def first_kernel(
    count, heads, inner, steps, late_tile,
    q_ref, late_q_ref, maps_ref, k_ref, v_ref, key_map_ref,
    qf_ref, late_soft_ref, kf_ref, rim_k_ref, rim_v_ref, prefix_ref,
    v_ones, outer_mask, local_sum, sums, halo, sum_send, sum_recv, halo_send, halo_recv,
):
    step = pl.program_id(0)
    rank = lax.axis_index("seq")
    tokens, hd = k_ref.shape
    rows = outer_mask.shape[0]

    def halo_copy(i):
        return pltpu.make_async_remote_copy(
            src_ref=(k_ref, v_ref)[i].at[pl.ds(tokens - W, W)],
            dst_ref=halo.at[i],
            send_sem=halo_send.at[i],
            recv_sem=halo_recv.at[i],
            device_id={"seq": rank + 1},
            device_id_type=MESH,
        )

    def sum_copy(k):
        return pltpu.make_async_remote_copy(
            src_ref=local_sum,
            dst_ref=sums.at[k - 1],
            send_sem=sum_send.at[k - 1],
            recv_sem=sum_recv.at[k - 1],
            device_id={"seq": rank + k},
            device_id_type=MESH,
        )

    @pl.when(step == 0)
    def _():
        barrier = seq_barrier(rank, count)
        kf_ref[...] = nn(k_ref[...], key_map_ref[...]).astype(jnp.bfloat16)
        local_sum[...] = tn(kf_ref[...], v_ref[...])
        outer_mask[...] = head_masks(rows, heads, inner, hd)[0]
        v_ones[:, :hd] = v_ref[...]
        v_ones[:, hd:] = jnp.ones((tokens, hd), jnp.bfloat16)
        pl.semaphore_wait(barrier, count - 1)
        for k in range(1, count):
            @pl.when(rank + k < count)
            def _():
                sum_copy(k).start()
        @pl.when(rank + 1 < count)
        def _():
            halo_copy(0).start()
            halo_copy(1).start()

    outer = heads // inner
    maps = jnp.concatenate(
        [
            jnp.concatenate([maps_ref[(a * inner + b) * hd : (a * inner + b + 1) * hd] for b in range(inner)], 1)
            for a in range(outer)
        ], 0
    )
    inner_head = lax.broadcasted_iota(jnp.int32, (rows, hd), 0) % inner
    for start in range(0, q_ref.shape[0], rows):
        q = q_ref[start : start + rows, :]
        spread = nn(jnp.concatenate([q] * outer, 1) * outer_mask[...], maps)
        qf = spread[:, :hd]
        for b in range(1, inner):
            qf = jnp.where(inner_head == b, spread[:, b * hd : (b + 1) * hd], qf)
        qf_ref[start : start + rows, :] = qf.astype(jnp.bfloat16)

    tile_rows = TILE * heads
    tiles = late_q_ref.shape[0] // tile_rows
    for tile in range(tiles):
        first = pl.multiple_of((late_tile + step * tiles + tile) * TILE - W, TILE)
        k_win = k_ref[pl.ds(first, W + TILE), :]
        v_win = v_ones[pl.ds(first, W + TILE), :]
        for sub in range(0, tile_rows, rows):
            start = tile * tile_rows + sub
            late_soft_ref[start : start + rows, :] = window_softmax(
                late_q_ref[start : start + rows, :], k_win, v_win, ahead_of(rows, sub, heads)[1]
            )

    @pl.when(step == steps - 1)
    def _():
        prefix_ref[...] = jnp.zeros_like(prefix_ref)
        for k in range(1, count):
            @pl.when(rank + k < count)
            def _():
                sum_copy(k).wait_send()
            @pl.when(rank >= k)
            def _():
                sum_copy(k).wait_recv()
                prefix_ref[...] += sums[k - 1]
        @pl.when(rank + 1 < count)
        def _():
            halo_copy(0).wait_send()
            halo_copy(1).wait_send()
        @pl.when(rank >= 1)
        def _():
            halo_copy(0).wait_recv()
            halo_copy(1).wait_recv()
            rim_k_ref[...] = halo[0]
            rim_v_ref[...] = halo[1]
        @pl.when(rank == 0)
        def _():
            rim_k_ref[...] = jnp.zeros_like(rim_k_ref)
            rim_v_ref[...] = jnp.zeros_like(rim_v_ref)


def last_kernel(count, g_ref, g16_ref, out_ref, slots, send_sem, recv_sem):
    rank = lax.axis_index("seq")
    barrier = seq_barrier(rank, count)
    pl.semaphore_wait(barrier, count - 1)
    copies = []
    for k in range(1, count):
        target = lax.rem(rank + k, count)
        copies.append(pltpu.make_async_remote_copy(
            src_ref=g16_ref.at[target],
            dst_ref=slots.at[k - 1],
            send_sem=send_sem.at[k - 1],
            recv_sem=recv_sem.at[k - 1],
            device_id={"seq": target},
            device_id_type=MESH,
        ))
    for copy in copies:
        copy.start()
    total = g_ref[rank]
    for k, copy in enumerate(copies):
        copy.wait()
        total = total + slots[k].astype(jnp.float32)
    hd = out_ref.shape[2]
    for h in range(out_ref.shape[1]):
        out_ref[:, h, :] = total[:, h * hd : (h + 1) * hd]


def main_kernel(
    tokens_here, heads, inner, tiles, rows_sub, steps, early,
    q_ref, qf_ref, c_ref, late_soft_ref, k_ref, v_ref, kf_ref, rim_k_ref, rim_v_ref, prefix_ref,
    soft_ref, linear_ref, grad_ref, grad16_ref,
    k_ext, v_ext, outer_mask, inner_mask, state, grad,
):
    step = pl.program_id(0)
    rank = lax.axis_index("seq")
    hd = q_ref.shape[1]
    rows = TILE * heads
    outer = heads // inner

    @pl.when(step == 0)
    def _():
        k_ext[:W] = rim_k_ref[...]
        k_ext[W:] = k_ref[...]
        v_ext[:W, :hd] = rim_v_ref[...]
        v_ext[W:, :hd] = v_ref[...]
        v_ext[:, hd:] = jnp.ones((v_ext.shape[0], hd), jnp.bfloat16)
        outer_mask[...], inner_mask[...] = head_masks(rows_sub, heads, inner, hd)
        state[...] = prefix_ref[...]
        grad[...] = jnp.zeros_like(grad)

    zero = jnp.zeros((TILE, hd), jnp.bfloat16)
    mids = W // TILE

    def block(with_softmax):
        for tile in range(tiles):
            index = step * tiles + tile
            first = pl.multiple_of(index * TILE, TILE)
            k_win = k_ext[pl.ds(first, W + TILE), :]
            v_win = v_ext[pl.ds(first, W + TILE), :]
            kf = kf_ref[pl.ds(first, TILE), :]
            v = v_ref[pl.ds(first, TILE), :]
            s_now = state[...]

            def diagonal(a, b):
                return jnp.concatenate(
                    [jnp.concatenate([a, zero], 1), jnp.concatenate([zero, b], 1)], 0
                )

            into_scores = diagonal(kf, v)
            carried = diagonal(s_now.astype(jnp.bfloat16), s_now.T.astype(jnp.bfloat16))
            from_scores = jnp.concatenate([diagonal(v, kf), carried], 0)
            invalid = [
                jnp.where((rank == 0) & (index + j < mids), -1e30, 0.0).astype(jnp.float32)
                for j in range(mids)
            ]
            queries, gradients = [], []
            for sub in range(rows // rows_sub):
                start = tile * rows + sub * rows_sub
                q = q_ref[start : start + rows_sub, :]
                c = c_ref[start : start + rows_sub, :]
                local, ahead = ahead_of(rows_sub, sub * rows_sub, heads)
                if with_softmax:
                    soft_ref[start : start + rows_sub, :] = window_softmax(q, k_win, v_win, ahead, invalid)
                pair = jnp.concatenate([qf_ref[start : start + rows_sub, :], c], 1)
                pair_scores = nt(pair, into_scores)
                ahead_two = jnp.concatenate([ahead, ahead], 1)
                pair_scores = jnp.where(ahead_two, 0.0, pair_scores).astype(jnp.bfloat16)
                pair_out = nn(jnp.concatenate([pair_scores, pair], 1), from_scores)
                position = rank * tokens_here + index * TILE + local + 1
                factor = lax.rsqrt(position.astype(jnp.float32))
                linear_ref[start : start + rows_sub, :] = (factor * pair_out[:, :hd]).astype(jnp.bfloat16)
                fg = (factor * pair_out[:, hd:]).astype(jnp.bfloat16)
                queries.append(jnp.concatenate([q] * outer, 1) * outer_mask[...])
                gradients.append(jnp.concatenate([fg] * inner, 1) * inner_mask[...])
            grad[...] += tn(jnp.concatenate(queries, 0), jnp.concatenate(gradients, 0))
            state[...] = s_now + tn(kf, v)

    @pl.when(step < early)
    def _():
        block(True)

    @pl.when(step >= early)
    def _():
        soft_ref[...] = late_soft_ref[...]
        block(False)

    @pl.when(step == steps - 1)
    def _():
        for a in range(outer):
            block = grad[a * hd : (a + 1) * hd, :]
            block = block.reshape(grad_ref.shape[:2] + (inner * hd,))
            grad_ref[:, :, a * inner * hd : (a + 1) * inner * hd] = block
            grad16_ref[:, :, a * inner * hd : (a + 1) * inner * hd] = block.astype(jnp.bfloat16)


def per_device(queries, keys, values, query_maps, key_map, linear_cotangent):
    tokens_here, hd = keys.shape
    heads = queries.shape[1]
    count = lax.axis_size("seq")
    inner = 2 if heads % 2 == 0 else 1
    outer = heads // inner
    share = hd // count
    tiles = 4
    rows_sub = min(512, TILE * heads)
    step_rows = TILE * tiles * heads
    total = tokens_here * heads
    steps = total // step_rows
    early = steps // 2
    late_rows = (steps - early) * step_rows // steps
    whole = lambda a: pl.BlockSpec(a.shape, lambda i: (0,) * len(a.shape))
    rows_spec = pl.BlockSpec((step_rows, hd), lambda i: (i, 0))
    maps = query_maps.reshape(heads * hd, hd)
    queries = queries.reshape(total, hd)
    cotangent = linear_cotangent.reshape(total, hd)

    rows16 = jax.ShapeDtypeStruct((total, hd), jnp.bfloat16)
    late16 = jax.ShapeDtypeStruct((steps * late_rows, hd), jnp.bfloat16)
    kf16 = jax.ShapeDtypeStruct((tokens_here, hd), jnp.bfloat16)
    rim = jax.ShapeDtypeStruct((W, hd), jnp.bfloat16)
    square = jax.ShapeDtypeStruct((hd, hd), jnp.float32)
    dma = pltpu.SemaphoreType.DMA
    query_features, late_soft, key_features, rim_keys, rim_values, prefix = pl.pallas_call(
        functools.partial(first_kernel, count, heads, inner, steps, early * tiles),
        grid=(steps,),
        in_specs=[rows_spec, pl.BlockSpec((late_rows, hd), lambda i: (i + early * step_rows // late_rows, 0))]
        + [whole(a) for a in (maps, keys, values, key_map)],
        out_specs=[rows_spec, pl.BlockSpec((late_rows, hd), lambda i: (i, 0))]
        + [whole(a) for a in (kf16, rim, rim, square)],
        out_shape=[rows16, late16, kf16, rim, rim, square],
        scratch_shapes=[
            pltpu.VMEM((tokens_here, 2 * hd), jnp.bfloat16),
            pltpu.VMEM((rows_sub, outer * hd), jnp.bfloat16),
            pltpu.VMEM((hd, hd), jnp.float32),
            pltpu.VMEM((count - 1, hd, hd), jnp.float32),
            pltpu.VMEM((2, W, hd), jnp.bfloat16),
            dma((count - 1,)), dma((count - 1,)), dma((2,)), dma((2,)),
        ],
        compiler_params=pltpu.CompilerParams(
            dimension_semantics=("arbitrary",), collective_id=0, has_side_effects=True
        ),
        name="features",
    )(queries, queries, maps, keys, values, key_map)

    pieces = (count, share, heads * hd)
    small = (keys, values, key_features, rim_keys, rim_values, prefix)
    soft, linear, grad, grad16 = pl.pallas_call(
        functools.partial(main_kernel, tokens_here, heads, inner, tiles, rows_sub, steps, early),
        grid=(steps,),
        in_specs=[rows_spec] * 3
        + [pl.BlockSpec((step_rows, hd), lambda i: (jnp.maximum(i - early, 0), 0))]
        + [whole(a) for a in small],
        out_specs=[rows_spec] * 2 + [pl.BlockSpec(pieces, lambda i: (0, 0, 0))] * 2,
        out_shape=[
            rows16, rows16,
            jax.ShapeDtypeStruct(pieces, jnp.float32),
            jax.ShapeDtypeStruct(pieces, jnp.bfloat16),
        ],
        scratch_shapes=[
            pltpu.VMEM((tokens_here + W, hd), jnp.bfloat16),
            pltpu.VMEM((tokens_here + W, 2 * hd), jnp.bfloat16),
            pltpu.VMEM((rows_sub, outer * hd), jnp.bfloat16),
            pltpu.VMEM((rows_sub, inner * hd), jnp.bfloat16),
            pltpu.VMEM((hd, hd), jnp.float32),
            pltpu.VMEM((outer * hd, inner * hd), jnp.float32),
        ],
        compiler_params=pltpu.CompilerParams(dimension_semantics=("arbitrary",)),
        name="attention",
    )(queries, query_features, cotangent, late_soft, *small)

    vmem = pl.BlockSpec(memory_space=pltpu.VMEM)
    mine = pl.pallas_call(
        functools.partial(last_kernel, count),
        in_specs=[vmem, vmem],
        out_specs=vmem,
        out_shape=jax.ShapeDtypeStruct((share, heads, hd), jnp.float32),
        scratch_shapes=[
            pltpu.VMEM((count - 1,) + pieces[1:], jnp.bfloat16), dma((count - 1,)), dma((count - 1,)),
        ],
        compiler_params=pltpu.CompilerParams(collective_id=1, has_side_effects=True),
        name="map_gradient",
    )(grad, grad16)
    shape = (tokens_here, heads, hd)
    return soft.reshape(shape), linear.reshape(shape), mine


def solution(mesh):
    rows = P(("groups", "seq"), ("head", "rep"), None)
    return jax.shard_map(
        per_device,
        mesh=mesh,
        in_specs=(
            rows,
            P(("groups", "seq"), None),
            P(("groups", "seq"), None),
            P(("groups", "head", "rep"), None, None),
            P("groups", None),
            rows,
        ),
        out_specs=(rows, rows, rows),
        check_vma=False,
    )
```

profile of v0, /device:TPU:0, one launch (start us, length us, event | category | flops | bytes accessed | tf_op | source)
XLA Modules:
  0.0 57.7 jit_solution(3533731852223571415)
XLA Ops:
  0.6 20.9 %features.1 = (bf16[16384,128]{1,0:T(8,128)(2,1)}, bf16[8192,128]{1,0:T(8,128)(2,1)}, bf16[4096,128]{1,0:T(8,128)(2,1)}, bf16[512,128]{1,0:T(8,128)(2,1)}, bf16[512,128]{1,0:T(8,128)(2,1)}, /*index=5*/f32[128,128]{1,0:T(8,128)}) custom-call(bf16[16384,128]{1,0:T(8,128)(2,1)} %bitcast.5, bf16[16384,128]{1,0:T(8,128)(2,1)} %bitcast.6, ...), custom_call_target="tpu_custom_call" | custom-call | tf_op jit(solution)/shard_map/features/pallas_call | solution.py:316
  21.5 27.3 %attention.1 = (bf16[16384,128]{1,0:T(8,128)(2,1)}, bf16[16384,128]{1,0:T(8,128)(2,1)}, f32[4,32,512]{2,1,0:T(8,128)}, bf16[4,32,512]{2,1,0:T(8,128)(2,1)}) custom-call(bf16[16384,128]{1,0:T(8,128)(2,1)} %bitcast.7, bf16[16384,128]{1,0:T(8,128)(2,1)} %get-tuple-element.13.qf_ref, bf16[16384,128]{1,0:T(8,128)(2,1)} %bitcast.8, ...), custom_call_target="tpu_custom_call" | custom-call | tf_op jit(solution)/shard_map/attention/pallas_call | solution.py:340
  48.8 7.4 %map_gradient.1 = f32[32,4,128]{2,1,0:T(4,128)} custom-call(f32[4,32,512]{2,1,0:T(8,128)} %get-tuple-element.21.g_ref, bf16[4,32,512]{2,1,0:T(8,128)(2,1)} %get-tuple-element.22.g16_ref), custom_call_target="tpu_custom_call" | custom-call | tf_op jit(solution)/shard_map/map_gradient/pallas_call | solution.py:365
  56.2 1.5 %copy.10 = f32[32,4,128]{2,1,0:T(4,128)} copy(f32[32,4,128]{2,1,0:T(4,128)} %map_gradient.1) | data formatting | bytes 131072
where the time goes:
time: 57.9 us; the launch traced here: 57.7 us
  Pallas kernels  55.6 us (96%)
  local copies, waits for them, and re-layouts  1.47 us (3%)
  between operations  0.65 us (1%)
    pallas_call x1, Pallas kernels, per_device(): pl.pallas_call(functools.partial(main_kernel, tokens_here, heads, inner,...  27.3 us
    pallas_call x1, Pallas kernels, per_device(): pl.pallas_call(functools.partial(first_kernel, count, heads, inner, steps...  20.9 us
    pallas_call x1, Pallas kernels, per_device(): pl.pallas_call(functools.partial(last_kernel, count), in_specs=[vmem, vme...  7.43 us
    unnamed x1, local copies, waits for them, and re-layouts  1.47 us

commit v1 on v0

v1 whole, which is shorter than its diff:
```python
import functools

import jax
import jax.numpy as jnp
from jax import lax
from jax.experimental import pallas as pl
from jax.experimental.pallas import tpu as pltpu
from jax.sharding import PartitionSpec as P

W = 512
TILE = 128
MIDS = W // TILE
ONES = 16
MESH = pl.DeviceIdType.MESH
F32 = jnp.float32
BF16 = jnp.bfloat16


def nt(a, b):
    return lax.dot_general(a, b, (((1,), (1,)), ((), ())), preferred_element_type=F32)


def nn(a, b):
    return jnp.dot(a, b, preferred_element_type=F32)


def beside(parts):
    return parts[0] if len(parts) == 1 else jnp.concatenate(parts, 1)


def below(parts):
    return parts[0] if len(parts) == 1 else jnp.concatenate(parts, 0)


def later_key(heads):
    shape = (TILE, heads * TILE)
    return lax.broadcasted_iota(jnp.int32, shape, 0) > lax.broadcasted_iota(jnp.int32, shape, 1) % TILE


def heads_apart(ref):
    return pltpu.einshape("tha->hta", ref[...])


def tile_of(x, tile):
    rows = slice(tile * TILE, (tile + 1) * TILE)
    return below([x[h, rows] for h in range(x.shape[0])])


def head_cols(x):
    return [x[:, h : h + TILE] for h in range(0, x.shape[1], TILE)]


def heads_together(tiles):
    heads = tiles[0].shape[1] // TILE
    rows = [below([head_cols(t)[h].T for t in tiles])[None] for h in range(heads)]
    return pltpu.einshape("hta->tha", below(rows))


def scale_of(rank, tokens_here, first, heads):
    token = lax.broadcasted_iota(jnp.int32, (1, TILE), 1) + (rank * tokens_here + first + 1)
    return beside([lax.rsqrt(token.astype(F32))] * heads)


def softmax_weights(scores, ahead, hd):
    scale = hd ** (-0.5) * 1.4426950408889634
    parts = [scores[j * TILE : (j + 1) * TILE] for j in range(MIDS + 1)]
    kept = [jnp.where(ahead, parts[0], parts[MIDS])] + parts[1:MIDS]
    highest = jnp.max(functools.reduce(jnp.maximum, kept), axis=0, keepdims=True)
    kept = [jnp.exp2((p - highest) * scale) for p in kept]
    return below(
        [jnp.where(ahead, kept[0], 0.0).astype(BF16)]
        + [p.astype(BF16) for p in kept[1:]]
        + [jnp.where(ahead, 0.0, kept[0]).astype(BF16)]
    )


def softmax_tiles(q_ref, k_ext, v_ext, out_ref, first_tile, tiles, ahead):
    hd = q_ref.shape[2]
    q = heads_apart(q_ref)

    def scores(t):
        first = pl.multiple_of((first_tile + t) * TILE, TILE)
        return nt(k_ext[pl.ds(first, W + TILE), :], tile_of(q, t))

    def output(t, weights):
        values = beside([v_ext[first_tile + t + j] for j in range(MIDS + 1)])
        out = nn(values, weights)
        return (out[:hd] * (1.0 / out[hd : hd + 1])).astype(BF16)

    done, weights = [], None
    now = scores(0)
    for t in range(tiles):
        after = scores(t + 1) if t + 1 < tiles else None
        fresh = softmax_weights(now, ahead, hd)
        if weights is not None:
            done.append(output(t - 1, weights))
        now, weights = after, fresh
    done.append(output(tiles - 1, weights))
    out_ref[...] = heads_together(done)


def first_kernel(
    count, tokens_here, tiles, before, middle, steps,
    q_ref, c_ref, k_ref, v_ref, key_map_ref,
    soft_ref, kf_ref, vt_ref, prefix_ref, mine_ref,
    k_ext, v_ext, kft, local_sum, sums, halo, state, grad, pieces, pieces16, slots,
    sum_send, sum_recv, halo_send, halo_recv, piece_send, piece_recv,
):
    step = pl.program_id(0)
    rank = lax.axis_index("seq")
    heads, hd = q_ref.shape[1:]
    blocks = tokens_here // TILE
    share = hd // count
    barrier = pltpu.get_barrier_semaphore()

    def halo_copy(i):
        return pltpu.make_async_remote_copy(
            src_ref=(k_ref, v_ref)[i].at[pl.ds(tokens_here - W, W)],
            dst_ref=halo.at[i],
            send_sem=halo_send.at[i],
            recv_sem=halo_recv.at[i],
            device_id={"seq": rank + 1},
            device_id_type=MESH,
        )

    def sum_copy(k):
        return pltpu.make_async_remote_copy(
            src_ref=local_sum,
            dst_ref=sums.at[k - 1],
            send_sem=sum_send.at[k - 1],
            recv_sem=sum_recv.at[k - 1],
            device_id={"seq": rank + k},
            device_id_type=MESH,
        )

    def piece_copy(k):
        target = lax.rem(rank + k, count)
        return pltpu.make_async_remote_copy(
            src_ref=pieces16.at[target],
            dst_ref=slots.at[k - 1],
            send_sem=piece_send.at[k - 1],
            recv_sem=piece_recv.at[k - 1],
            device_id={"seq": target},
            device_id_type=MESH,
        )

    @pl.when(step == 0)
    def _():
        for k in range(1, count):
            pl.semaphore_signal(
                barrier, inc=1, device_id={"seq": lax.rem(rank + k, count)}, device_id_type=MESH
            )
        key_map_t = key_map_ref[...].astype(F32).T.astype(BF16)
        kft[...] = nt(key_map_t, k_ref[...]).astype(BF16)
        local_sum[...] = nn(kft[...], v_ref[...]).astype(BF16)
        kf_ref[...] = nn(k_ref[...], key_map_ref[...]).astype(BF16)
        k_ext[W:] = k_ref[...]
        for b in range(blocks):
            turned = v_ref[b * TILE : (b + 1) * TILE, :].T
            vt_ref[b] = turned
            v_ext[MIDS + b, :hd] = turned
        v_ext[MIDS:, hd:] = jnp.ones((blocks, ONES, TILE), BF16)
        grad[...] = jnp.zeros_like(grad)

    @pl.when(step == 1)
    def _():
        pl.semaphore_wait(barrier, count - 1)
        for k in range(1, count):
            @pl.when(rank + k < count)
            def _():
                sum_copy(k).start()
        @pl.when(rank + 1 < count)
        def _():
            halo_copy(0).start()
            halo_copy(1).start()

    @pl.when(step == before)
    def _():
        state[...] = jnp.zeros_like(state)
        for k in range(1, count):
            @pl.when(rank + k < count)
            def _():
                sum_copy(k).wait_send()
            @pl.when(rank >= k)
            def _():
                sum_copy(k).wait_recv()
                state[...] += sums[k - 1].astype(F32)
        prefix_ref[...] = state[...].T

    @pl.when(step == before + middle)
    def _():
        for h in range(heads):
            turned = grad[h].T
            for p in range(count):
                piece = turned[p * share : (p + 1) * share]
                pieces[p, :, h * hd : (h + 1) * hd] = piece
                pieces16[p, :, h * hd : (h + 1) * hd] = piece.astype(BF16)
        for k in range(1, count):
            piece_copy(k).start()

    @pl.when(step == steps - 1)
    def _():
        @pl.when(rank + 1 < count)
        def _():
            halo_copy(0).wait_send()
            halo_copy(1).wait_send()
        @pl.when(rank >= 1)
        def _():
            halo_copy(0).wait_recv()
            halo_copy(1).wait_recv()
            k_ext[:W] = halo[0]
            for b in range(MIDS):
                v_ext[b, :hd] = halo[1, b * TILE : (b + 1) * TILE, :].T
                v_ext[b, hd:] = jnp.ones((ONES, TILE), BF16)
        @pl.when(rank == 0)
        def _():
            k_ext[:W] = jnp.broadcast_to(k_ref[0:1, :], (W, hd))
            v_ext[:MIDS] = jnp.zeros((MIDS,) + v_ext.shape[1:], BF16)

    ahead = later_key(heads)

    @pl.when((step < before) | (step >= before + middle))
    def _():
        place = jnp.where(step < before, steps - middle - 1 - step, steps - 1 - step)
        softmax_tiles(q_ref, k_ext, v_ext, soft_ref, place * tiles, tiles, ahead)

    @pl.when((step >= before) & (step < before + middle))
    def _():
        base = (step - before) * tiles
        q = heads_apart(q_ref)
        c = heads_apart(c_ref)
        starts = []
        now = state[...]
        for t in range(tiles):
            starts.append(now.astype(BF16))
            first = pl.multiple_of((base + t) * TILE, TILE)
            now = now + nn(kft[:, pl.ds(first, TILE)], v_ref[pl.ds(first, TILE), :])
        state[...] = now

        turned = [tile_of(c, t).T for t in range(tiles)]

        def scores(t):
            first = pl.multiple_of((base + t) * TILE, TILE)
            back = nn(v_ref[pl.ds(first, TILE), :], turned[t])
            return jnp.where(ahead, 0.0, back).astype(BF16)

        def gradient(t, back):
            first = pl.multiple_of((base + t) * TILE, TILE)
            out = nn(beside([kft[:, pl.ds(first, TILE)], starts[t]]), below([back, turned[t]]))
            return (out * scale_of(rank, tokens_here, first, heads)).astype(BF16)

        backs = [scores(t) for t in range(tiles)]
        found = [head_cols(gradient(t, backs[t])) for t in range(tiles)]
        for h in range(heads):
            grad[h] += nn(beside([found[t][h] for t in range(tiles)]), q[h])

    @pl.when(step == steps - 1)
    def _():
        total = pieces[rank]
        for k in range(1, count):
            piece_copy(k).wait()
            total = total + slots[k - 1].astype(F32)
        mine_ref[...] = total


def last_kernel(
    tokens_here, tiles, steps,
    q_ref, soft_in_ref, maps_ref, kf_ref, vt_ref, prefix_ref, mine_in_ref,
    soft_ref, linear_ref, mine_ref,
    maps_t, state,
):
    step = pl.program_id(0)
    rank = lax.axis_index("seq")
    heads, hd = q_ref.shape[1:]

    @pl.when(step == 0)
    def _():
        for h in range(heads):
            maps_t[h] = maps_ref[h].T
            mine_ref[:, h, :] = mine_in_ref[:, h * hd : (h + 1) * hd]
        state[...] = prefix_ref[...]

    soft_ref[...] = soft_in_ref[...]
    ahead = later_key(heads)
    q = heads_apart(q_ref)
    base = step * tiles
    starts = []
    now = state[...]
    for t in range(tiles):
        starts.append(now.astype(BF16))
        first = pl.multiple_of((base + t) * TILE, TILE)
        now = now + nn(vt_ref[base + t], kf_ref[pl.ds(first, TILE), :])
    state[...] = now

    features = [nt(maps_t[h], q[h]).astype(BF16) for h in range(heads)]
    turned = [beside([head_cols(f)[t] for f in features]) for t in range(tiles)]

    def scores(t):
        first = pl.multiple_of((base + t) * TILE, TILE)
        return jnp.where(ahead, 0.0, nn(kf_ref[pl.ds(first, TILE), :], turned[t])).astype(BF16)

    def output(t, inside):
        first = (base + t) * TILE
        out = nn(beside([vt_ref[base + t], starts[t]]), below([inside, turned[t]]))
        return (out * scale_of(rank, tokens_here, first, heads)).astype(BF16)

    insides = [scores(t) for t in range(tiles)]
    linear_ref[...] = heads_together([output(t, insides[t]) for t in range(tiles)])


def per_device(queries, keys, values, query_maps, key_map, linear_cotangent):
    tokens_here, hd = keys.shape
    heads = queries.shape[1]
    count = lax.axis_size("seq")
    share = hd // count
    tiles = 4
    step_tokens = TILE * tiles
    middle = tokens_here // step_tokens
    before = middle // 2
    steps = 2 * middle
    blocks = tokens_here // TILE
    once = lambda a: pl.BlockSpec(a.shape, lambda i: (0,) * len(a.shape), pipeline_mode=pl.Buffered(1))
    block = lambda index: pl.BlockSpec((step_tokens, heads, hd), lambda i: (index(i), 0, 0))
    dma = pltpu.SemaphoreType.DMA

    def soft_place(i):
        held = jnp.where(i < before + middle, middle - before, steps - 1 - i)
        return jnp.where(i < before, middle - 1 - i, held)

    def middle_place(i):
        return jnp.clip(i - before, 0, middle - 1)

    def query_place(i):
        return jnp.where((i >= before) & (i < before + middle), i - before, soft_place(i))

    rows16 = jax.ShapeDtypeStruct((tokens_here, heads, hd), BF16)
    kf16 = jax.ShapeDtypeStruct((tokens_here, hd), BF16)
    vt16 = jax.ShapeDtypeStruct((blocks, hd, TILE), BF16)
    square = jax.ShapeDtypeStruct((hd, hd), F32)
    piece = jax.ShapeDtypeStruct((share, heads * hd), F32)
    soft, key_features, values_t, prefix, mine = pl.pallas_call(
        functools.partial(first_kernel, count, tokens_here, tiles, before, middle, steps),
        grid=(steps,),
        in_specs=[block(query_place), block(middle_place)] + [once(a) for a in (keys, values, key_map)],
        out_specs=[block(soft_place)] + [once(a) for a in (kf16, vt16, square, piece)],
        out_shape=[rows16, kf16, vt16, square, piece],
        scratch_shapes=[
            pltpu.VMEM((tokens_here + W, hd), BF16),
            pltpu.VMEM((blocks + MIDS, hd + ONES, TILE), BF16),
            pltpu.VMEM((hd, tokens_here), BF16),
            pltpu.VMEM((hd, hd), BF16),
            pltpu.VMEM((count - 1, hd, hd), BF16),
            pltpu.VMEM((2, W, hd), BF16),
            pltpu.VMEM((hd, hd), F32),
            pltpu.VMEM((heads, hd, hd), F32),
            pltpu.VMEM((count, share, heads * hd), F32),
            pltpu.VMEM((count, share, heads * hd), BF16),
            pltpu.VMEM((count - 1, share, heads * hd), BF16),
            dma((count - 1,)), dma((count - 1,)), dma((2,)), dma((2,)), dma((count - 1,)), dma((count - 1,)),
        ],
        compiler_params=pltpu.CompilerParams(
            dimension_semantics=("arbitrary",), collective_id=0, has_side_effects=True
        ),
        name="softmax_and_gradient",
    )(queries, linear_cotangent, keys, values, key_map)

    along = block(lambda i: i)
    small = (query_maps, key_features, values_t, prefix, mine)
    final = jax.ShapeDtypeStruct((share, heads, hd), F32)
    return pl.pallas_call(
        functools.partial(last_kernel, tokens_here, tiles, middle),
        grid=(middle,),
        in_specs=[along, along] + [once(a) for a in small],
        out_specs=[along, along, once(final)],
        out_shape=[rows16, rows16, final],
        scratch_shapes=[pltpu.VMEM((heads, hd, hd), BF16), pltpu.VMEM((hd, hd), F32)],
        compiler_params=pltpu.CompilerParams(dimension_semantics=("arbitrary",)),
        name="linear",
    )(queries, soft, *small)


def solution(mesh):
    rows = P(("groups", "seq"), ("head", "rep"), None)
    return jax.shard_map(
        per_device,
        mesh=mesh,
        in_specs=(
            rows,
            P(("groups", "seq"), None),
            P(("groups", "seq"), None),
            P(("groups", "head", "rep"), None, None),
            P("groups", None),
            rows,
        ),
        out_specs=(rows, rows, rows),
        check_vma=False,
    )
```

time: 57.9 us -> 46.6 us (0.80)
  Pallas kernels: 55.6 us -> 45.5 us
  local copies, waits for them, and re-layouts: 1.47 us -> 0 us
    pallas_call x3 -> x2, Pallas kernels: 55.6 us -> 45.5 us  [the longest x1 33.1 us: per_device(): pl.pallas_call(functools.partial(first_kernel, count, tokens_here, tiles,...]
    unnamed x1 -> x0, local copies, waits for them, and re-layouts: 1.47 us -> none
where the time goes in v1:
time: 46.6 us; the launch traced here: 46.1 us
  Pallas kernels  45.5 us (98%)
  between operations  0.64 us (1%)
    pallas_call x1, Pallas kernels, per_device(): pl.pallas_call(functools.partial(first_kernel, count, tokens_here, tiles,...  33.1 us
    pallas_call x1, Pallas kernels, per_device(): pl.pallas_call(functools.partial(last_kernel, tokens_here, tiles, middle)...  12.3 us

profile of v1, /device:TPU:0, one launch (start us, length us, event | category | flops | bytes accessed | tf_op | source)
XLA Modules:
  0.0 46.1 jit_solution(16669617204805795614)
XLA Ops:
  0.6 33.1 %softmax_and_gradient.1 = (bf16[4096,4,128]{2,1,0:T(4,128)(2,1)}, bf16[4096,128]{1,0:T(8,128)(2,1)}, bf16[32,128,128]{2,1,0:T(8,128)(2,1)}, f32[128,128]{1,0:T(8,128)}, f32[32,512]{1,0:T(8,128)}) custom-call(bf16[4096,4,128]{2,1,0:T(4,128)(2,1)} %q_ref.3, bf16[4096,4,128]{2,1,0:T(4,128)(2,1)} %c_ref.1, bf16[4096,128]{1,0:T(8,128)(2,1)} %k_ref.1, ...), custom_call_target="tpu_custom_call" | custom-call | tf_op jit(solution)/shard_map/softmax_and_gradient/pallas_call | solution.py:341
  33.8 12.3 %linear.1 = (bf16[4096,4,128]{2,1,0:T(4,128)(2,1)}, bf16[4096,4,128]{2,1,0:T(4,128)(2,1)}, f32[32,4,128]{2,1,0:T(4,128)}) custom-call(bf16[4096,4,128]{2,1,0:T(4,128)(2,1)} %q_ref.3, bf16[4096,4,128]{2,1,0:T(4,128)(2,1)} %get-tuple-element.8.soft_in_ref, bf16[4,128,128]{2,1,0:T(8,128)(2,1)} %maps_ref.1, bf16[4096,128]{1,0:T(8,128)(2,1)} %get-tuple-element.9.kf_ref, ...), custom_call_target="tpu_custom_call" | custom-call | tf_op jit(solution)/shard_map/linear/pallas_call | solution.py:370

commit v2 on v1

v2 whole, which is shorter than its diff:
```python
import functools

import jax
import jax.numpy as jnp
from jax import lax
from jax.experimental import pallas as pl
from jax.experimental.pallas import tpu as pltpu
from jax.sharding import PartitionSpec as P

W = 512
TILE = 128
MIDS = W // TILE
ONES = 16
MESH = pl.DeviceIdType.MESH
F32 = jnp.float32
BF16 = jnp.bfloat16


def nt(a, b):
    return lax.dot_general(a, b, (((1,), (1,)), ((), ())), preferred_element_type=F32)


def nn(a, b):
    return jnp.dot(a, b, preferred_element_type=F32)


def beside(parts):
    return parts[0] if len(parts) == 1 else jnp.concatenate(parts, 1)


def below(parts):
    return parts[0] if len(parts) == 1 else jnp.concatenate(parts, 0)


def later_key(heads):
    shape = (TILE, TILE)
    one = lax.broadcasted_iota(jnp.int32, shape, 0) > lax.broadcasted_iota(jnp.int32, shape, 1)
    return beside([one] * heads)


def later_key_in_band(heads):
    shape = (TILE // heads, TILE)
    return lax.broadcasted_iota(jnp.int32, shape, 0) > lax.broadcasted_iota(jnp.int32, shape, 1) // heads


def columns(x):
    return [x[:, h : h + TILE] for h in range(0, x.shape[1], TILE)]


def at_tile(tile, rows=TILE):
    return pl.ds(pl.multiple_of(tile * rows, rows), rows)


def head_rows(ref, tile, heads):
    if heads == 1:
        return [ref[at_tile(tile), :]]
    own = ref.at[at_tile(tile, TILE * heads), :]
    return [own[pl.ds(h, TILE, stride=heads), :] for h in range(heads)]


def scale_of(before, tile, heads):
    token = lax.broadcasted_iota(jnp.int32, (1, TILE), 1) + (before + tile * TILE + 1)
    return beside([lax.rsqrt(token.astype(F32))] * heads)


def softmax_weights(scores, heads, hd):
    scale = hd ** (-0.5) * 1.4426950408889634
    ahead = later_key_in_band(heads)
    span = TILE // heads
    found = []
    for g, own in enumerate(columns(scores)):
        parts = [own[j * TILE : (j + 1) * TILE] for j in range(MIDS + 1)]
        a, b = g * span, (g + 1) * span
        edge = [parts[MIDS][:a]] * (a > 0) + [jnp.where(ahead, parts[0][a:b], parts[MIDS][a:b])]
        kept = [below(edge + [parts[0][b:]] * (b < TILE))] + parts[1:MIDS]
        highest = jnp.max(functools.reduce(jnp.maximum, kept), axis=0, keepdims=True)
        kept = [jnp.exp2((p - highest) * scale) for p in kept]
        edge = kept[0]
        old = [jnp.zeros((a, TILE), BF16)] * (a > 0) + [jnp.where(ahead, edge[a:b], 0.0).astype(BF16)]
        new = [jnp.where(ahead, 0.0, edge[a:b]).astype(BF16)]
        if a > 0:
            new = [edge[:a].astype(BF16)] + new
        if b < TILE:
            old = old + [edge[b:].astype(BF16)]
            new = new + [jnp.zeros((TILE - b, TILE), BF16)]
        found.append(below(old + [p.astype(BF16) for p in kept[1:]] + new))
    return beside(found)


def softmax_tiles(q_ref, k_ext, v_ext, out_ref, first_tile, tiles, heads):
    hd = q_ref.shape[1]
    rows = TILE * heads

    def scores(t):
        keys = k_ext[pl.ds(pl.multiple_of((first_tile + t) * TILE, TILE), W + TILE), :]
        return nt(keys, q_ref[at_tile(first_tile + t, rows), :])

    def output(t, weights):
        values = beside([v_ext[first_tile + t + j] for j in range(MIDS + 1)])
        out = nn(values, weights)
        out_ref[at_tile(first_tile + t, rows), :] = (out[:hd] * (1.0 / out[hd : hd + 1])).astype(BF16).T

    weights, now = None, scores(0)
    for t in range(tiles):
        after = scores(t + 1) if t + 1 < tiles else None
        fresh = softmax_weights(now, heads, hd)
        if weights is not None:
            output(t - 1, weights)
        now, weights = after, fresh
    output(tiles - 1, weights)


def gradient_tiles(q_ref, c_ref, v_ref, kft, state, grad, before, first_tile, tiles):
    heads = grad.shape[0]
    ahead = later_key(heads)
    group = 2 if tiles % 2 == 0 else 1
    now = state[...]
    starts, turned, backs, found, q = {}, {}, {}, {}, {}

    def load(t, now):
        if t >= tiles:
            return now
        here = at_tile(first_tile + t)
        turned[t] = below(head_rows(c_ref, first_tile + t, heads)).T
        q[t] = head_rows(q_ref, first_tile + t, heads)
        starts[t] = now.astype(BF16)
        return now + nn(kft[:, here], v_ref[here, :])

    def score(t):
        if t < tiles:
            back = nn(v_ref[at_tile(first_tile + t), :], turned[t])
            backs[t] = jnp.where(ahead, 0.0, back).astype(BF16)

    def gradient(t):
        left = beside([kft[:, at_tile(first_tile + t)], starts[t]])
        out = nn(left, below([backs[t], turned[t]])) * scale_of(before, first_tile + t, heads)
        found[t] = columns(out.astype(BF16))

    def add(ts):
        for h in range(heads):
            grad[h] += nn(beside([found[t][h] for t in ts]), below([q[t][h] for t in ts]))

    now = load(1, load(0, now))
    score(0)
    for t in range(tiles):
        now = load(t + 2, now)
        score(t + 1)
        gradient(t)
        if t and t % group == 0:
            add(range(t - group, t))
    add(range(tiles - group, tiles))
    state[...] = now


def linear_tiles(q_ref, kf_ref, vt_ref, maps_t, state, out_ref, first_token):
    heads, hd = q_ref.shape[1:]
    tiles = q_ref.shape[0] // TILE
    ahead = later_key(heads)
    group = 2 if tiles % 2 == 0 else 1
    q = pltpu.einshape("tha->hta", q_ref[...])
    now = state[...]
    starts, turned, inside, done = {}, {}, {}, []

    def load(t, now):
        if t >= tiles:
            return now
        if t % group == 0:
            rows = slice(t * TILE, (t + group) * TILE)
            features = [columns(nt(maps_t[h], q[h, rows]).astype(BF16)) for h in range(heads)]
            for i in range(group):
                turned[t + i] = beside([f[i] for f in features])
        starts[t] = now.astype(BF16)
        return now + nn(vt_ref[t, :hd], kf_ref[at_tile(t), :])

    def score(t):
        if t < tiles:
            scores = nn(kf_ref[at_tile(t), :], turned[t])
            inside[t] = jnp.where(ahead, 0.0, scores).astype(BF16)

    def output(t):
        left = beside([vt_ref[t, :hd], starts[t]])
        out = nn(left, below([inside[t], turned[t]])) * scale_of(first_token, t, heads)
        done.append([x.T for x in columns(out.astype(BF16))])

    now = load(1, load(0, now))
    score(0)
    for t in range(tiles):
        now = load(t + 2, now)
        score(t + 1)
        output(t)
    state[...] = now
    out_ref[...] = pltpu.einshape("hta->tha", below([below([d[h] for d in done])[None] for h in range(heads)]))


def first_kernel(
    count, step_tiles,
    q_hbm, c_hbm, k_hbm, v_hbm, key_map_ref,
    soft_hbm, kf_hbm, vt_hbm, prefix_ref, mine_ref,
    q_all, c_all, k_ext, v_all, v_ext, kf, kft, soft_all,
    local_sum, sums, halo, state, grad, pieces, pieces16, slots,
    load_sem, store_sem, sum_send, sum_recv, halo_send, halo_recv, piece_send, piece_recv,
):
    rank = lax.axis_index("seq")
    heads, hd = grad.shape[:2]
    tokens_here = v_all.shape[0]
    blocks = tokens_here // TILE
    share = hd // count
    half = blocks // 2
    before = rank * tokens_here

    def halo_copy(i):
        return pltpu.make_async_remote_copy(
            src_ref=(k_ext.at[pl.ds(tokens_here, W)], v_all.at[pl.ds(tokens_here - W, W)])[i],
            dst_ref=halo.at[i],
            send_sem=halo_send.at[i],
            recv_sem=halo_recv.at[i],
            device_id={"seq": rank + 1},
            device_id_type=MESH,
        )

    def sum_copy(k):
        return pltpu.make_async_remote_copy(
            src_ref=local_sum,
            dst_ref=sums.at[k - 1],
            send_sem=sum_send.at[k - 1],
            recv_sem=sum_recv.at[k - 1],
            device_id={"seq": rank + k},
            device_id_type=MESH,
        )

    def piece_copy(k):
        target = lax.rem(rank + k, count)
        return pltpu.make_async_remote_copy(
            src_ref=pieces16.at[target],
            dst_ref=slots.at[k - 1],
            send_sem=piece_send.at[k - 1],
            recv_sem=piece_recv.at[k - 1],
            device_id={"seq": target},
            device_id_type=MESH,
        )

    rows = TILE * heads
    late, soon = pl.ds(half * rows, (blocks - half) * rows), pl.ds(0, half * rows)
    loads = [
        pltpu.make_async_copy(source, target, load_sem.at[i])
        for i, (source, target) in enumerate([
            (k_hbm, k_ext.at[pl.ds(W, tokens_here)]),
            (v_hbm, v_all),
            (q_hbm.at[late], q_all.at[late]),
            (c_hbm, c_all),
            (q_hbm.at[soon], q_all.at[soon]),
        ])
    ]
    barrier = pltpu.get_barrier_semaphore()
    for k in range(1, count):
        pl.semaphore_signal(barrier, inc=1, device_id={"seq": lax.rem(rank + k, count)}, device_id_type=MESH)
    for load in loads[:3]:
        load.start()
    loads[0].wait()
    key_map_t = key_map_ref[...].astype(F32).T.astype(BF16)
    kft[...] = nt(key_map_t, k_ext[W:]).astype(BF16)
    kf[...] = nn(k_ext[W:], key_map_ref[...]).astype(BF16)
    loads[1].wait()
    local_sum[...] = nn(kft[...], v_all[...]).astype(BF16)
    for b in range(blocks):
        v_ext[MIDS + b, :hd] = v_all[b * TILE : (b + 1) * TILE, :].T
    v_ext[MIDS:, hd:] = jnp.ones((blocks, ONES, TILE), BF16)
    grad[...] = jnp.zeros_like(grad)
    state[...] = jnp.zeros_like(state)
    for load in loads[3:]:
        load.start()
    stores = [
        pltpu.make_async_copy(kf, kf_hbm, store_sem.at[0]),
        pltpu.make_async_copy(v_ext.at[pl.ds(MIDS, blocks)], vt_hbm, store_sem.at[1]),
        pltpu.make_async_copy(soft_all.at[late], soft_hbm.at[late], store_sem.at[2]),
        pltpu.make_async_copy(soft_all.at[soon], soft_hbm.at[soon], store_sem.at[3]),
    ]
    stores[0].start()
    stores[1].start()
    loads[2].wait()

    def softmax(first_tile, tiles):
        softmax_tiles(q_all, k_ext, v_ext, soft_all, first_tile, tiles, heads)

    lead = step_tiles // 2
    softmax(half, lead)

    pl.semaphore_wait(barrier, count - 1)
    for k in range(1, count):
        @pl.when(rank + k < count)
        def _():
            sum_copy(k).start()
    @pl.when(rank + 1 < count)
    def _():
        halo_copy(0).start()
        halo_copy(1).start()

    rest = (half - lead) // 2
    @pl.loop(0, 2)
    def _(i):
        softmax(half + lead + i * rest, rest)

    stores[2].start()
    for k in range(1, count):
        @pl.when(rank + k < count)
        def _():
            sum_copy(k).wait_send()
        @pl.when(rank >= k)
        def _():
            sum_copy(k).wait_recv()
            state[...] += sums[k - 1].astype(F32)
    prefix_ref[...] = state[...].T
    loads[3].wait()
    loads[4].wait()

    @pl.loop(0, blocks // step_tiles)
    def _(i):
        gradient_tiles(q_all, c_all, v_all, kft, state, grad, before, i * step_tiles, step_tiles)

    for h in range(heads):
        turned = grad[h].T
        for p in range(count):
            piece = turned[p * share : (p + 1) * share]
            pieces[p, :, h * hd : (h + 1) * hd] = piece
            pieces16[p, :, h * hd : (h + 1) * hd] = piece.astype(BF16)
    for k in range(1, count):
        piece_copy(k).start()

    @pl.loop(0, half // step_tiles)
    def _(i):
        @pl.when(i == half // step_tiles - 1)
        def _():
            @pl.when(rank + 1 < count)
            def _():
                halo_copy(0).wait_send()
                halo_copy(1).wait_send()
            @pl.when(rank >= 1)
            def _():
                halo_copy(0).wait_recv()
                halo_copy(1).wait_recv()
                k_ext[:W] = halo[0]
                for b in range(MIDS):
                    v_ext[b, :hd] = halo[1, b * TILE : (b + 1) * TILE, :].T
                    v_ext[b, hd:] = jnp.ones((ONES, TILE), BF16)
            @pl.when(rank == 0)
            def _():
                k_ext[:W] = jnp.broadcast_to(k_ext[W : W + 1, :], (W, hd))
                v_ext[:MIDS] = jnp.zeros((MIDS,) + v_ext.shape[1:], BF16)
        softmax(half - (i + 1) * step_tiles, step_tiles)

    stores[3].start()
    total = pieces[rank]
    for k in range(1, count):
        piece_copy(k).wait()
        total = total + slots[k - 1].astype(F32)
    mine_ref[...] = total
    for store in stores:
        store.wait()


def last_kernel(
    steps,
    q_ref, kf_ref, vt_ref, soft_in_hbm, maps_ref, prefix_ref, mine_in_ref,
    linear_ref, soft_hbm, mine_ref,
    soft_all, maps_t, state, load_sem, store_sem,
):
    step = pl.program_id(0)
    heads, hd = q_ref.shape[1:]
    step_tokens = q_ref.shape[0]
    rows = step_tokens * heads

    def part(i):
        return pl.ds(pl.multiple_of(i * rows, rows), rows)

    def load(i):
        return pltpu.make_async_copy(soft_in_hbm.at[part(i)], soft_all.at[part(i)], load_sem.at[i])

    def store(i):
        return pltpu.make_async_copy(soft_all.at[part(i)], soft_hbm.at[part(i)], store_sem.at[i])

    @pl.when(step == 0)
    def _():
        for i in range(steps):
            load(i).start()
        for h in range(heads):
            maps_t[h] = maps_ref[h].T
            mine_ref[:, h, :] = mine_in_ref[:, h * hd : (h + 1) * hd]
        state[...] = prefix_ref[...]

    @pl.when(step >= 1)
    def _():
        load(step - 1).wait()
        store(step - 1).start()

    @pl.when(step == steps - 1)
    def _():
        load(step).wait()
        store(step).start()

    first_token = (lax.axis_index("seq") * steps + step) * step_tokens
    linear_tiles(q_ref, kf_ref, vt_ref, maps_t, state, linear_ref, first_token)

    @pl.when(step == steps - 1)
    def _():
        for i in range(steps):
            store(i).wait()


def per_device(queries, keys, values, query_maps, key_map, linear_cotangent):
    tokens_here, hd = keys.shape
    heads = queries.shape[1]
    count = lax.axis_size("seq")
    share = hd // count
    blocks = tokens_here // TILE
    step_tiles = 8
    steps = blocks // step_tiles
    flat = (tokens_here * heads, hd)
    dma = pltpu.SemaphoreType.DMA
    hbm = pl.BlockSpec(memory_space=pl.ANY)
    vmem = pl.BlockSpec(memory_space=pltpu.VMEM)

    rows16 = jax.ShapeDtypeStruct(flat, BF16)
    kf16 = jax.ShapeDtypeStruct((tokens_here, hd), BF16)
    vt16 = jax.ShapeDtypeStruct((blocks, hd + ONES, TILE), BF16)
    square = jax.ShapeDtypeStruct((hd, hd), F32)
    piece = jax.ShapeDtypeStruct((share, heads * hd), F32)
    soft, key_features, values_t, prefix, mine = pl.pallas_call(
        functools.partial(first_kernel, count, step_tiles),
        in_specs=[hbm, hbm, hbm, hbm, vmem],
        out_specs=[hbm, hbm, hbm, vmem, vmem],
        out_shape=[rows16, kf16, vt16, square, piece],
        scratch_shapes=[
            pltpu.VMEM(flat, BF16),
            pltpu.VMEM(flat, BF16),
            pltpu.VMEM((tokens_here + W, hd), BF16),
            pltpu.VMEM((tokens_here, hd), BF16),
            pltpu.VMEM((blocks + MIDS, hd + ONES, TILE), BF16),
            pltpu.VMEM((tokens_here, hd), BF16),
            pltpu.VMEM((hd, tokens_here), BF16),
            pltpu.VMEM(flat, BF16),
            pltpu.VMEM((hd, hd), BF16),
            pltpu.VMEM((count - 1, hd, hd), BF16),
            pltpu.VMEM((2, W, hd), BF16),
            pltpu.VMEM((hd, hd), F32),
            pltpu.VMEM((heads, hd, hd), F32),
            pltpu.VMEM((count, share, heads * hd), F32),
            pltpu.VMEM((count, share, heads * hd), BF16),
            pltpu.VMEM((count - 1, share, heads * hd), BF16),
            dma((5,)), dma((4,)),
            dma((count - 1,)), dma((count - 1,)), dma((2,)), dma((2,)), dma((count - 1,)), dma((count - 1,)),
        ],
        compiler_params=pltpu.CompilerParams(collective_id=0, has_side_effects=True),
        name="softmax_and_gradient",
    )(queries.reshape(flat), linear_cotangent.reshape(flat), keys, values, key_map)

    once = lambda a: pl.BlockSpec(a.shape, lambda i: (0,) * len(a.shape), pipeline_mode=pl.Buffered(1))
    tokens = step_tiles * TILE
    along = pl.BlockSpec((tokens, heads, hd), lambda i: (i, 0, 0))
    final = jax.ShapeDtypeStruct((share, heads, hd), F32)
    linear, soft, mine = pl.pallas_call(
        functools.partial(last_kernel, steps),
        grid=(steps,),
        in_specs=[
            along,
            pl.BlockSpec((tokens, hd), lambda i: (i, 0)),
            pl.BlockSpec((step_tiles, hd + ONES, TILE), lambda i: (i, 0, 0)),
            hbm, once(query_maps), once(prefix), once(mine),
        ],
        out_specs=[along, hbm, once(final)],
        out_shape=[jax.ShapeDtypeStruct((tokens_here, heads, hd), BF16), rows16, final],
        scratch_shapes=[
            pltpu.VMEM(flat, BF16),
            pltpu.VMEM((heads, hd, hd), BF16),
            pltpu.VMEM((hd, hd), F32),
            dma((steps,)), dma((steps,)),
        ],
        compiler_params=pltpu.CompilerParams(dimension_semantics=("arbitrary",)),
        name="linear",
    )(queries, key_features, values_t, soft, query_maps, prefix, mine)
    return soft.reshape(queries.shape), linear, mine


def solution(mesh):
    rows = P(("groups", "seq"), ("head", "rep"), None)
    return jax.shard_map(
        per_device,
        mesh=mesh,
        in_specs=(
            rows,
            P(("groups", "seq"), None),
            P(("groups", "seq"), None),
            P(("groups", "head", "rep"), None, None),
            P("groups", None),
            rows,
        ),
        out_specs=(rows, rows, rows),
        check_vma=False,
    )
```

time: 46.6 us -> 38.1 us (0.82)
  Pallas kernels: 45.5 us -> 37.1 us
    pallas_call x2, Pallas kernels: 45.5 us -> 37.1 us  [the longest x1 26.9 us: per_device(): pl.pallas_call(functools.partial(first_kernel, count, step_tiles), in_spe...]
where the time goes in v2:
time: 38.1 us; the launch traced here: 37.9 us
  Pallas kernels  37.1 us (97%)
  between operations  0.8 us (2%)
    pallas_call x1, Pallas kernels, per_device(): pl.pallas_call(functools.partial(first_kernel, count, step_tiles), in_spe...  26.9 us
    pallas_call x1, Pallas kernels, per_device(): pl.pallas_call(functools.partial(last_kernel, steps), grid=(steps,), in_s...  10.1 us

profile of v2, /device:TPU:0, one launch (start us, length us, event | category | flops | bytes accessed | tf_op | source)
XLA Modules:
  0.0 37.9 jit_solution(14543274853895727087)
XLA Ops:
  0.6 26.9 %softmax_and_gradient.1 = (bf16[16384,128]{1,0:T(8,128)(2,1)}, bf16[4096,128]{1,0:T(8,128)(2,1)}, bf16[32,144,128]{2,1,0:T(8,128)(2,1)}, f32[128,128]{1,0:T(8,128)}, f32[32,512]{1,0:T(8,128)}) custom-call(bf16[16384,128]{1,0:T(8,128)(2,1)} %bitcast.3, bf16[16384,128]{1,0:T(8,128)(2,1)} %bitcast.4, bf16[4096,128]{1,0:T(8,128)(2,1)} %k_hbm.1, ...), custom_call_target="tpu_custom_call" | custom-call | tf_op jit(solution)/shard_map/softmax_and_gradient/pallas_call | solution.py:427
  27.6 10.1 %linear.1 = (bf16[4096,4,128]{2,1,0:T(4,128)(2,1)}, bf16[16384,128]{1,0:T(8,128)(2,1)}, f32[32,4,128]{2,1,0:T(4,128)}) custom-call(bf16[4096,4,128]{2,1,0:T(4,128)(2,1)} %q_ref.1, bf16[4096,128]{1,0:T(8,128)(2,1)} %get-tuple-element.11.kf_ref, bf16[32,144,128]{2,1,0:T(8,128)(2,1)} %get-tuple-element.12.vt_ref, ...), custom_call_target="tpu_custom_call" | custom-call | tf_op jit(solution)/shard_map/linear/pallas_call | solution.py:460

commit v3 on v2

--- a/solution.py
+++ b/solution.py
@@ -68,39 +68,59 @@
     ahead = later_key_in_band(heads)
     span = TILE // heads
     found = []
-    for g, own in enumerate(columns(scores)):
-        parts = [own[j * TILE : (j + 1) * TILE] for j in range(MIDS + 1)]
-        a, b = g * span, (g + 1) * span
-        edge = [parts[MIDS][:a]] * (a > 0) + [jnp.where(ahead, parts[0][a:b], parts[MIDS][a:b])]
-        kept = [below(edge + [parts[0][b:]] * (b < TILE))] + parts[1:MIDS]
-        highest = jnp.max(functools.reduce(jnp.maximum, kept), axis=0, keepdims=True)
-        kept = [jnp.exp2((p - highest) * scale) for p in kept]
-        edge = kept[0]
-        old = [jnp.zeros((a, TILE), BF16)] * (a > 0) + [jnp.where(ahead, edge[a:b], 0.0).astype(BF16)]
-        new = [jnp.where(ahead, 0.0, edge[a:b]).astype(BF16)]
-        if a > 0:
-            new = [edge[:a].astype(BF16)] + new
-        if b < TILE:
-            old = old + [edge[b:].astype(BF16)]
-            new = new + [jnp.zeros((TILE - b, TILE), BF16)]
-        found.append(below(old + [p.astype(BF16) for p in kept[1:]] + new))
-    return beside(found)
-
-
-def softmax_tiles(q_ref, k_ext, v_ext, out_ref, first_tile, tiles, heads):
+    for part, chunk in enumerate(scores):
+        skipped = part * (chunk.shape[0] - W)
+        for i, own in enumerate(columns(chunk)):
+            a = skipped + i * span
+            b = a + span
+            rows = lambda start, stop: own[start - skipped : stop - skipped]
+            edge = [rows(W, W + a)] * (a > 0) + [jnp.where(ahead, rows(a, b), rows(W + a, W + b))]
+            edge = below(edge + [rows(b, TILE)] * (b < TILE))
+            kept = [edge] + [rows(j * TILE, (j + 1) * TILE) for j in range(1, MIDS)]
+            highest = jnp.max(functools.reduce(jnp.maximum, kept), axis=0, keepdims=True)
+            kept = [jnp.exp2((p - highest) * scale) for p in kept]
+            edge = kept[0]
+            old = [jnp.zeros((a, TILE), BF16)] * (a > 0) + [jnp.where(ahead, edge[a:b], 0.0).astype(BF16)]
+            new = [jnp.where(ahead, 0.0, edge[a:b]).astype(BF16)]
+            if a > 0:
+                new = [edge[:a].astype(BF16)] + new
+            if b < TILE:
+                old = old + [edge[b:].astype(BF16)]
+                new = new + [jnp.zeros((TILE - b, TILE), BF16)]
+            total = jnp.sum(functools.reduce(jnp.add, kept), axis=0, keepdims=True)
+            found.append((below(old + [p.astype(BF16) for p in kept[1:]] + new), total))
+    return beside([f[0] for f in found]), beside([f[1] for f in found])
+
+
+def softmax_tiles(q_ref, k_ext, v_ext, out_ref, first_tile, tiles, heads, present, meanwhile, stored):
     hd = q_ref.shape[1]
     rows = TILE * heads
+    lanes = min(2 * TILE, rows)
+    span = lanes // heads
 
     def scores(t):
-        keys = k_ext[pl.ds(pl.multiple_of((first_tile + t) * TILE, TILE), W + TILE), :]
-        return nt(keys, q_ref[at_tile(first_tile + t, rows), :])
-
-    def output(t, weights):
+        found = []
+        for i in range(rows // lanes):
+            keys = k_ext[pl.ds(pl.multiple_of((first_tile + t) * TILE + i * span, span), W + span), :]
+            queries = q_ref[pl.ds(pl.multiple_of((first_tile + t) * rows + i * lanes, lanes), lanes), :]
+            found.append(nt(keys, queries))
+        return found
+
+    def output(t, found):
+        weights, total = found
         values = beside([v_ext[first_tile + t + j] for j in range(MIDS + 1)])
+        if present is not None and t < MIDS:
+            ones = jnp.ones((ONES, TILE), BF16)
+            values = below([values, beside([present if t + j < MIDS else ones for j in range(MIDS + 1)])])
         out = nn(values, weights)
-        out_ref[at_tile(first_tile + t, rows), :] = (out[:hd] * (1.0 / out[hd : hd + 1])).astype(BF16).T
+        if present is not None and t < MIDS:
+            total = out[hd : hd + 1]
+        out_ref[at_tile(first_tile + t, rows), :] = (out[:hd] * (1.0 / total)).astype(BF16).T
+        stored(t)
 
     weights, now = None, scores(0)
+    if meanwhile is not None:
+        meanwhile()
     for t in range(tiles):
         after = scores(t + 1) if t + 1 < tiles else None
         fresh = softmax_weights(now, heads, hd)
@@ -170,7 +190,7 @@
             for i in range(group):
                 turned[t + i] = beside([f[i] for f in features])
         starts[t] = now.astype(BF16)
-        return now + nn(vt_ref[t, :hd], kf_ref[at_tile(t), :])
+        return now + nn(vt_ref[t], kf_ref[at_tile(t), :])
 
     def score(t):
         if t < tiles:
@@ -178,7 +198,7 @@
             inside[t] = jnp.where(ahead, 0.0, scores).astype(BF16)
 
     def output(t):
-        left = beside([vt_ref[t, :hd], starts[t]])
+        left = beside([vt_ref[t], starts[t]])
         out = nn(left, below([inside[t], turned[t]])) * scale_of(first_token, t, heads)
         done.append([x.T for x in columns(out.astype(BF16))])
 
@@ -195,8 +215,8 @@
 def first_kernel(
     count, step_tiles,
     q_hbm, c_hbm, k_hbm, v_hbm, key_map_ref,
-    soft_hbm, kf_hbm, vt_hbm, prefix_ref, mine_ref,
-    q_all, c_all, k_ext, v_all, v_ext, kf, kft, soft_all,
+    soft_hbm, vt_hbm, prefix_ref, mine_ref,
+    q_all, c_all, k_ext, v_all, v_ext, kft, soft_all,
     local_sum, sums, halo, state, grad, pieces, pieces16, slots,
     load_sem, store_sem, sum_send, sum_recv, halo_send, halo_recv, piece_send, piece_recv,
 ):
@@ -240,50 +260,59 @@
         )
 
     rows = TILE * heads
-    late, soon = pl.ds(half * rows, (blocks - half) * rows), pl.ds(0, half * rows)
+    lead = step_tiles // 2
+
+    def tiles_of(first, tiles):
+        return pl.ds(first * rows, tiles * rows)
+
+    first_part, late, soon = tiles_of(half, lead), tiles_of(half + lead, blocks - half - lead), tiles_of(0, half)
     loads = [
         pltpu.make_async_copy(source, target, load_sem.at[i])
         for i, (source, target) in enumerate([
             (k_hbm, k_ext.at[pl.ds(W, tokens_here)]),
             (v_hbm, v_all),
+            (q_hbm.at[first_part], q_all.at[first_part]),
             (q_hbm.at[late], q_all.at[late]),
             (c_hbm, c_all),
             (q_hbm.at[soon], q_all.at[soon]),
         ])
     ]
+
+    def soft_store(i):
+        part = tiles_of(i * lead, lead)
+        return pltpu.make_async_copy(soft_all.at[part], soft_hbm.at[part], store_sem.at[i])
+
+    def softmax(first_tile, tiles, present=None, meanwhile=None):
+        def stored(t):
+            if (t + 1) % lead == 0:
+                soft_store((first_tile + t) // lead).start()
+
+        softmax_tiles(q_all, k_ext, v_ext, soft_all, first_tile, tiles, heads, present, meanwhile, stored)
+
     barrier = pltpu.get_barrier_semaphore()
     for k in range(1, count):
         pl.semaphore_signal(barrier, inc=1, device_id={"seq": lax.rem(rank + k, count)}, device_id_type=MESH)
     for load in loads[:3]:
         load.start()
-    loads[0].wait()
-    key_map_t = key_map_ref[...].astype(F32).T.astype(BF16)
-    kft[...] = nt(key_map_t, k_ext[W:]).astype(BF16)
-    kf[...] = nn(k_ext[W:], key_map_ref[...]).astype(BF16)
-    loads[1].wait()
-    local_sum[...] = nn(kft[...], v_all[...]).astype(BF16)
-    for b in range(blocks):
-        v_ext[MIDS + b, :hd] = v_all[b * TILE : (b + 1) * TILE, :].T
-    v_ext[MIDS:, hd:] = jnp.ones((blocks, ONES, TILE), BF16)
     grad[...] = jnp.zeros_like(grad)
     state[...] = jnp.zeros_like(state)
     for load in loads[3:]:
         load.start()
-    stores = [
-        pltpu.make_async_copy(kf, kf_hbm, store_sem.at[0]),
-        pltpu.make_async_copy(v_ext.at[pl.ds(MIDS, blocks)], vt_hbm, store_sem.at[1]),
-        pltpu.make_async_copy(soft_all.at[late], soft_hbm.at[late], store_sem.at[2]),
-        pltpu.make_async_copy(soft_all.at[soon], soft_hbm.at[soon], store_sem.at[3]),
-    ]
-    stores[0].start()
-    stores[1].start()
+    key_map_t = key_map_ref[...].astype(F32).T.astype(BF16)
+    loads[0].wait()
+    kft[...] = nt(key_map_t, k_ext[W:]).astype(BF16)
+    loads[1].wait()
     loads[2].wait()
-
-    def softmax(first_tile, tiles):
-        softmax_tiles(q_all, k_ext, v_ext, soft_all, first_tile, tiles, heads)
-
-    lead = step_tiles // 2
-    softmax(half, lead)
+    for b in range(blocks):
+        v_ext[MIDS + b] = v_all[b * TILE : (b + 1) * TILE, :].T
+
+    def shard_sum():
+        near, far = slice(0, tokens_here // 2), slice(tokens_here // 2, tokens_here)
+        local_sum[...] = (nn(kft[:, near], v_all[near, :]) + nn(kft[:, far], v_all[far, :])).astype(BF16)
+
+    softmax(half, lead, meanwhile=shard_sum)
+    vt_store = pltpu.make_async_copy(v_ext.at[pl.ds(MIDS, blocks)], vt_hbm, store_sem.at[blocks // lead])
+    vt_store.start()
 
     pl.semaphore_wait(barrier, count - 1)
     for k in range(1, count):
@@ -295,12 +324,9 @@
         halo_copy(0).start()
         halo_copy(1).start()
 
-    rest = (half - lead) // 2
-    @pl.loop(0, 2)
-    def _(i):
-        softmax(half + lead + i * rest, rest)
-
-    stores[2].start()
+    loads[3].wait()
+    softmax(half + lead, blocks - half - lead)
+
     for k in range(1, count):
         @pl.when(rank + k < count)
         def _():
@@ -310,12 +336,12 @@
             sum_copy(k).wait_recv()
             state[...] += sums[k - 1].astype(F32)
     prefix_ref[...] = state[...].T
-    loads[3].wait()
     loads[4].wait()
-
-    @pl.loop(0, blocks // step_tiles)
+    loads[5].wait()
+
+    @pl.loop(0, blocks // (2 * step_tiles))
     def _(i):
-        gradient_tiles(q_all, c_all, v_all, kft, state, grad, before, i * step_tiles, step_tiles)
+        gradient_tiles(q_all, c_all, v_all, kft, state, grad, before, i * 2 * step_tiles, 2 * step_tiles)
 
     for h in range(heads):
         turned = grad[h].T
@@ -326,43 +352,38 @@
     for k in range(1, count):
         piece_copy(k).start()
 
-    @pl.loop(0, half // step_tiles)
-    def _(i):
-        @pl.when(i == half // step_tiles - 1)
-        def _():
-            @pl.when(rank + 1 < count)
-            def _():
-                halo_copy(0).wait_send()
-                halo_copy(1).wait_send()
-            @pl.when(rank >= 1)
-            def _():
-                halo_copy(0).wait_recv()
-                halo_copy(1).wait_recv()
-                k_ext[:W] = halo[0]
-                for b in range(MIDS):
-                    v_ext[b, :hd] = halo[1, b * TILE : (b + 1) * TILE, :].T
-                    v_ext[b, hd:] = jnp.ones((ONES, TILE), BF16)
-            @pl.when(rank == 0)
-            def _():
-                k_ext[:W] = jnp.broadcast_to(k_ext[W : W + 1, :], (W, hd))
-                v_ext[:MIDS] = jnp.zeros((MIDS,) + v_ext.shape[1:], BF16)
-        softmax(half - (i + 1) * step_tiles, step_tiles)
-
-    stores[3].start()
+    @pl.when(rank + 1 < count)
+    def _():
+        halo_copy(0).wait_send()
+        halo_copy(1).wait_send()
+    @pl.when(rank >= 1)
+    def _():
+        halo_copy(0).wait_recv()
+        halo_copy(1).wait_recv()
+        k_ext[:W] = halo[0]
+        for b in range(MIDS):
+            v_ext[b] = halo[1, b * TILE : (b + 1) * TILE, :].T
+    @pl.when(rank == 0)
+    def _():
+        k_ext[:W] = jnp.broadcast_to(k_ext[W : W + 1, :], (W, hd))
+        v_ext[:MIDS] = jnp.zeros((MIDS,) + v_ext.shape[1:], BF16)
+    softmax(0, half, jnp.where(rank == 0, jnp.zeros((ONES, TILE), F32), 1.0).astype(BF16))
+
     total = pieces[rank]
     for k in range(1, count):
         piece_copy(k).wait()
         total = total + slots[k - 1].astype(F32)
     mine_ref[...] = total
-    for store in stores:
-        store.wait()
+    for i in range(blocks // lead):
+        soft_store(i).wait()
+    vt_store.wait()
 
 
 def last_kernel(
     steps,
-    q_ref, kf_ref, vt_ref, soft_in_hbm, maps_ref, prefix_ref, mine_in_ref,
+    q_ref, k_first_ref, k_next_ref, vt_ref, soft_in_hbm, key_map_ref, maps_ref, prefix_ref, mine_in_ref,
     linear_ref, soft_hbm, mine_ref,
-    soft_all, maps_t, state, load_sem, store_sem,
+    kf, soft_all, maps_t, state, load_sem, store_sem,
 ):
     step = pl.program_id(0)
     heads, hd = q_ref.shape[1:]
@@ -382,6 +403,7 @@
     def _():
         for i in range(steps):
             load(i).start()
+        kf[0] = nn(k_first_ref[...], key_map_ref[...]).astype(BF16)
         for h in range(heads):
             maps_t[h] = maps_ref[h].T
             mine_ref[:, h, :] = mine_in_ref[:, h * hd : (h + 1) * hd]
@@ -398,7 +420,8 @@
         store(step).start()
 
     first_token = (lax.axis_index("seq") * steps + step) * step_tokens
-    linear_tiles(q_ref, kf_ref, vt_ref, maps_t, state, linear_ref, first_token)
+    linear_tiles(q_ref, kf.at[lax.rem(step, 2)], vt_ref, maps_t, state, linear_ref, first_token)
+    kf[lax.rem(step + 1, 2)] = nn(k_next_ref[...], key_map_ref[...]).astype(BF16)
 
     @pl.when(step == steps - 1)
     def _():
@@ -420,22 +443,20 @@
     vmem = pl.BlockSpec(memory_space=pltpu.VMEM)
 
     rows16 = jax.ShapeDtypeStruct(flat, BF16)
-    kf16 = jax.ShapeDtypeStruct((tokens_here, hd), BF16)
-    vt16 = jax.ShapeDtypeStruct((blocks, hd + ONES, TILE), BF16)
+    vt16 = jax.ShapeDtypeStruct((blocks, hd, TILE), BF16)
     square = jax.ShapeDtypeStruct((hd, hd), F32)
     piece = jax.ShapeDtypeStruct((share, heads * hd), F32)
-    soft, key_features, values_t, prefix, mine = pl.pallas_call(
+    soft, values_t, prefix, mine = pl.pallas_call(
         functools.partial(first_kernel, count, step_tiles),
         in_specs=[hbm, hbm, hbm, hbm, vmem],
-        out_specs=[hbm, hbm, hbm, vmem, vmem],
-        out_shape=[rows16, kf16, vt16, square, piece],
+        out_specs=[hbm, hbm, vmem, vmem],
+        out_shape=[rows16, vt16, square, piece],
         scratch_shapes=[
             pltpu.VMEM(flat, BF16),
             pltpu.VMEM(flat, BF16),
             pltpu.VMEM((tokens_here + W, hd), BF16),
             pltpu.VMEM((tokens_here, hd), BF16),
-            pltpu.VMEM((blocks + MIDS, hd + ONES, TILE), BF16),
-            pltpu.VMEM((tokens_here, hd), BF16),
+            pltpu.VMEM((blocks + MIDS, hd, TILE), BF16),
             pltpu.VMEM((hd, tokens_here), BF16),
             pltpu.VMEM(flat, BF16),
             pltpu.VMEM((hd, hd), BF16),
@@ -446,7 +467,7 @@
             pltpu.VMEM((count, share, heads * hd), F32),
             pltpu.VMEM((count, share, heads * hd), BF16),
             pltpu.VMEM((count - 1, share, heads * hd), BF16),
-            dma((5,)), dma((4,)),
+            dma((6,)), dma((blocks // (step_tiles // 2) + 1,)),
             dma((count - 1,)), dma((count - 1,)), dma((2,)), dma((2,)), dma((count - 1,)), dma((count - 1,)),
         ],
         compiler_params=pltpu.CompilerParams(collective_id=0, has_side_effects=True),
@@ -462,13 +483,15 @@
         grid=(steps,),
         in_specs=[
             along,
-            pl.BlockSpec((tokens, hd), lambda i: (i, 0)),
-            pl.BlockSpec((step_tiles, hd + ONES, TILE), lambda i: (i, 0, 0)),
-            hbm, once(query_maps), once(prefix), once(mine),
+            pl.BlockSpec((tokens, hd), lambda i: (0, 0), pipeline_mode=pl.Buffered(1)),
+            pl.BlockSpec((tokens, hd), lambda i: (jnp.minimum(i + 1, steps - 1), 0)),
+            pl.BlockSpec((step_tiles, hd, TILE), lambda i: (i, 0, 0)),
+            hbm, once(key_map), once(query_maps), once(prefix), once(mine),
         ],
         out_specs=[along, hbm, once(final)],
         out_shape=[jax.ShapeDtypeStruct((tokens_here, heads, hd), BF16), rows16, final],
         scratch_shapes=[
+            pltpu.VMEM((2, tokens, hd), BF16),
             pltpu.VMEM(flat, BF16),
             pltpu.VMEM((heads, hd, hd), BF16),
             pltpu.VMEM((hd, hd), F32),
@@ -476,7 +499,7 @@
         ],
         compiler_params=pltpu.CompilerParams(dimension_semantics=("arbitrary",)),
         name="linear",
-    )(queries, key_features, values_t, soft, query_maps, prefix, mine)
+    )(queries, keys, keys, values_t, soft, key_map, query_maps, prefix, mine)
     return soft.reshape(queries.shape), linear, mine
 
 

time: 38.1 us -> 35.2 us (0.924)
  Pallas kernels: 37.1 us -> 34.1 us
    pallas_call x1, Pallas kernels: 26.9 us -> 24.3 us  [per_device(): pl.pallas_call(functools.partial(first_kernel, count, step_tiles), in_spe...]
where the time goes in v3:
time: 35.2 us; the launch traced here: 34.9 us
  Pallas kernels  34.1 us (97%)
  between operations  0.8 us (2%)
    pallas_call x1, Pallas kernels, per_device(): pl.pallas_call(functools.partial(first_kernel, count, step_tiles), in_spe...  24.3 us
    pallas_call x1, Pallas kernels, per_device(): pl.pallas_call(functools.partial(last_kernel, steps), grid=(steps,), in_s...  9.84 us

profile of v3, /device:TPU:0, one launch (start us, length us, event | category | flops | bytes accessed | tf_op | source)
XLA Modules:
  0.0 34.9 jit_solution(10394062283137282822)
XLA Ops:
  0.6 24.3 %softmax_and_gradient.1 = (bf16[16384,128]{1,0:T(8,128)(2,1)}, bf16[32,128,128]{2,1,0:T(8,128)(2,1)}, f32[128,128]{1,0:T(8,128)}, f32[32,512]{1,0:T(8,128)}) custom-call(bf16[16384,128]{1,0:T(8,128)(2,1)} %bitcast.3, bf16[16384,128]{1,0:T(8,128)(2,1)} %bitcast.4, bf16[4096,128]{1,0:T(8,128)(2,1)} %k_next_ref.1, bf16[4096,128]{1,0:T(8,128)(2,1)} %v_hbm.1, ...), custom_call_target="tpu_custom_call" | custom-call | tf_op jit(solution)/shard_map/softmax_and_gradient/pallas_call | solution.py:449
  24.9 9.8 %linear.1 = (bf16[4096,4,128]{2,1,0:T(4,128)(2,1)}, bf16[16384,128]{1,0:T(8,128)(2,1)}, f32[32,4,128]{2,1,0:T(4,128)}) custom-call(bf16[4096,4,128]{2,1,0:T(4,128)(2,1)} %q_ref.1, bf16[4096,128]{1,0:T(8,128)(2,1)} %k_next_ref.1, bf16[4096,128]{1,0:T(8,128)(2,1)} %k_next_ref.1, bf16[32,128,128]{2,1,0:T(8,128)(2,1)} %get-tuple-element.10.vt_ref, ...), custom_call_target="tpu_custom_call" | custom-call | tf_op jit(solution)/shard_map/linear/pallas_call | solution.py:481

commit v4 on v3

--- a/solution.py
+++ b/solution.py
@@ -11,6 +11,9 @@
 TILE = 128
 MIDS = W // TILE
 ONES = 16
+LAG = 3
+DEPTH = 2
+LATE = 1
 MESH = pl.DeviceIdType.MESH
 F32 = jnp.float32
 BF16 = jnp.bfloat16
@@ -63,32 +66,31 @@
     return beside([lax.rsqrt(token.astype(F32))] * heads)
 
 
-def softmax_weights(scores, heads, hd):
+def softmax_weights(chunk, part, heads, hd):
     scale = hd ** (-0.5) * 1.4426950408889634
     ahead = later_key_in_band(heads)
     span = TILE // heads
+    skipped = part * (chunk.shape[0] - W)
     found = []
-    for part, chunk in enumerate(scores):
-        skipped = part * (chunk.shape[0] - W)
-        for i, own in enumerate(columns(chunk)):
-            a = skipped + i * span
-            b = a + span
-            rows = lambda start, stop: own[start - skipped : stop - skipped]
-            edge = [rows(W, W + a)] * (a > 0) + [jnp.where(ahead, rows(a, b), rows(W + a, W + b))]
-            edge = below(edge + [rows(b, TILE)] * (b < TILE))
-            kept = [edge] + [rows(j * TILE, (j + 1) * TILE) for j in range(1, MIDS)]
-            highest = jnp.max(functools.reduce(jnp.maximum, kept), axis=0, keepdims=True)
-            kept = [jnp.exp2((p - highest) * scale) for p in kept]
-            edge = kept[0]
-            old = [jnp.zeros((a, TILE), BF16)] * (a > 0) + [jnp.where(ahead, edge[a:b], 0.0).astype(BF16)]
-            new = [jnp.where(ahead, 0.0, edge[a:b]).astype(BF16)]
-            if a > 0:
-                new = [edge[:a].astype(BF16)] + new
-            if b < TILE:
-                old = old + [edge[b:].astype(BF16)]
-                new = new + [jnp.zeros((TILE - b, TILE), BF16)]
-            total = jnp.sum(functools.reduce(jnp.add, kept), axis=0, keepdims=True)
-            found.append((below(old + [p.astype(BF16) for p in kept[1:]] + new), total))
+    for i, own in enumerate(columns(chunk)):
+        a = skipped + i * span
+        b = a + span
+        rows = lambda start, stop: own[start - skipped : stop - skipped]
+        edge = [rows(W, W + a)] * (a > 0) + [jnp.where(ahead, rows(a, b), rows(W + a, W + b))]
+        edge = below(edge + [rows(b, TILE)] * (b < TILE))
+        kept = [edge] + [rows(j * TILE, (j + 1) * TILE) for j in range(1, MIDS)]
+        highest = jnp.max(functools.reduce(jnp.maximum, kept), axis=0, keepdims=True)
+        kept = [jnp.exp2((p - highest) * scale) for p in kept]
+        edge = kept[0]
+        old = [jnp.zeros((a, TILE), BF16)] * (a > 0) + [jnp.where(ahead, edge[a:b], 0.0).astype(BF16)]
+        new = [jnp.where(ahead, 0.0, edge[a:b]).astype(BF16)]
+        if a > 0:
+            new = [edge[:a].astype(BF16)] + new
+        if b < TILE:
+            old = old + [edge[b:].astype(BF16)]
+            new = new + [jnp.zeros((TILE - b, TILE), BF16)]
+        total = jnp.sum(functools.reduce(jnp.add, kept), axis=0, keepdims=True)
+        found.append((below(old + [p.astype(BF16) for p in kept[1:]] + new), total))
     return beside([f[0] for f in found]), beside([f[1] for f in found])
 
 
@@ -98,36 +100,47 @@
     lanes = min(2 * TILE, rows)
     span = lanes // heads
 
-    def scores(t):
-        found = []
-        for i in range(rows // lanes):
-            keys = k_ext[pl.ds(pl.multiple_of((first_tile + t) * TILE + i * span, span), W + span), :]
-            queries = q_ref[pl.ds(pl.multiple_of((first_tile + t) * rows + i * lanes, lanes), lanes), :]
-            found.append(nt(keys, queries))
-        return found
-
-    def output(t, found):
+    chunks = rows // lanes
+    units = tiles * chunks
+    values = {}
+
+    def scores(u):
+        t, i = divmod(u, chunks)
+        if t >= tiles:
+            return None
+        keys = k_ext[pl.ds(pl.multiple_of((first_tile + t) * TILE + i * span, span), W + span), :]
+        queries = q_ref[pl.ds(pl.multiple_of((first_tile + t) * rows + i * lanes, lanes), lanes), :]
+        return nt(keys, queries)
+
+    def output(u, found):
+        t, i = divmod(u, chunks)
         weights, total = found
-        values = beside([v_ext[first_tile + t + j] for j in range(MIDS + 1)])
-        if present is not None and t < MIDS:
-            ones = jnp.ones((ONES, TILE), BF16)
-            values = below([values, beside([present if t + j < MIDS else ones for j in range(MIDS + 1)])])
-        out = nn(values, weights)
+        if i == 0:
+            values[t] = beside([v_ext[first_tile + t + j] for j in range(MIDS + 1)])
+            if present is not None and t < MIDS:
+                ones = jnp.ones((ONES, TILE), BF16)
+                sides = [present if t + j < MIDS else ones for j in range(MIDS + 1)]
+                values[t] = below([values[t], beside(sides)])
+        out = nn(values[t], weights)
         if present is not None and t < MIDS:
             total = out[hd : hd + 1]
-        out_ref[at_tile(first_tile + t, rows), :] = (out[:hd] * (1.0 / total)).astype(BF16).T
-        stored(t)
-
-    weights, now = None, scores(0)
+        out = (out[:hd] * (1.0 / total)).astype(BF16).T
+        out_ref[pl.ds(pl.multiple_of((first_tile + t) * rows + i * lanes, lanes), lanes), :] = out
+        if i == chunks - 1:
+            stored(t)
+
+    ahead, behind = DEPTH * chunks, LATE * chunks
+    now = {u: scores(u) for u in range(ahead)}
     if meanwhile is not None:
         meanwhile()
-    for t in range(tiles):
-        after = scores(t + 1) if t + 1 < tiles else None
-        fresh = softmax_weights(now, heads, hd)
-        if weights is not None:
-            output(t - 1, weights)
-        now, weights = after, fresh
-    output(tiles - 1, weights)
+    found = {}
+    for u in range(units):
+        now[u + ahead] = scores(u + ahead)
+        found[u] = softmax_weights(now.pop(u), u % chunks, heads, hd)
+        if u >= behind:
+            output(u - behind, found.pop(u - behind))
+    for u in range(units - behind, units):
+        output(u, found.pop(u))
 
 
 def gradient_tiles(q_ref, c_ref, v_ref, kft, state, grad, before, first_tile, tiles):
@@ -160,11 +173,13 @@
         for h in range(heads):
             grad[h] += nn(beside([found[t][h] for t in ts]), below([q[t][h] for t in ts]))
 
-    now = load(1, load(0, now))
-    score(0)
+    for t in range(LAG + 1):
+        now = load(t, now)
+    for t in range(LAG):
+        score(t)
     for t in range(tiles):
-        now = load(t + 2, now)
-        score(t + 1)
+        now = load(t + LAG + 1, now)
+        score(t + LAG)
         gradient(t)
         if t and t % group == 0:
             add(range(t - group, t))
@@ -202,11 +217,13 @@
         out = nn(left, below([inside[t], turned[t]])) * scale_of(first_token, t, heads)
         done.append([x.T for x in columns(out.astype(BF16))])
 
-    now = load(1, load(0, now))
-    score(0)
+    for t in range(LAG + 1):
+        now = load(t, now)
+    for t in range(LAG):
+        score(t)
     for t in range(tiles):
-        now = load(t + 2, now)
-        score(t + 1)
+        now = load(t + LAG + 1, now)
+        score(t + LAG)
         output(t)
     state[...] = now
     out_ref[...] = pltpu.einshape("hta->tha", below([below([d[h] for d in done])[None] for h in range(heads)]))
@@ -260,7 +277,8 @@
         )
 
     rows = TILE * heads
-    lead = step_tiles // 2
+    lead = 3 * step_tiles // 4
+    grain = 2
 
     def tiles_of(first, tiles):
         return pl.ds(first * rows, tiles * rows)
@@ -279,13 +297,13 @@
     ]
 
     def soft_store(i):
-        part = tiles_of(i * lead, lead)
+        part = tiles_of(i * grain, grain)
         return pltpu.make_async_copy(soft_all.at[part], soft_hbm.at[part], store_sem.at[i])
 
     def softmax(first_tile, tiles, present=None, meanwhile=None):
         def stored(t):
-            if (t + 1) % lead == 0:
-                soft_store((first_tile + t) // lead).start()
+            if (t + 1) % grain == 0:
+                soft_store((first_tile + t) // grain).start()
 
         softmax_tiles(q_all, k_ext, v_ext, soft_all, first_tile, tiles, heads, present, meanwhile, stored)
 
@@ -311,7 +329,7 @@
         local_sum[...] = (nn(kft[:, near], v_all[near, :]) + nn(kft[:, far], v_all[far, :])).astype(BF16)
 
     softmax(half, lead, meanwhile=shard_sum)
-    vt_store = pltpu.make_async_copy(v_ext.at[pl.ds(MIDS, blocks)], vt_hbm, store_sem.at[blocks // lead])
+    vt_store = pltpu.make_async_copy(v_ext.at[pl.ds(MIDS, blocks)], vt_hbm, store_sem.at[blocks // grain])
     vt_store.start()
 
     pl.semaphore_wait(barrier, count - 1)
@@ -374,7 +392,7 @@
         piece_copy(k).wait()
         total = total + slots[k - 1].astype(F32)
     mine_ref[...] = total
-    for i in range(blocks // lead):
+    for i in range(blocks // grain):
         soft_store(i).wait()
     vt_store.wait()
 
@@ -467,7 +485,7 @@
             pltpu.VMEM((count, share, heads * hd), F32),
             pltpu.VMEM((count, share, heads * hd), BF16),
             pltpu.VMEM((count - 1, share, heads * hd), BF16),
-            dma((6,)), dma((blocks // (step_tiles // 2) + 1,)),
+            dma((6,)), dma((blocks // 2 + 1,)),
             dma((count - 1,)), dma((count - 1,)), dma((2,)), dma((2,)), dma((count - 1,)), dma((count - 1,)),
         ],
         compiler_params=pltpu.CompilerParams(collective_id=0, has_side_effects=True),

time: 35.2 us -> 34 us (0.966)
  the two profiles are of different devices: /device:TPU:0 before, /device:TPU:16 now
where the time goes in v4:
time: 34 us; the launch traced here: 33.8 us
  Pallas kernels  33 us (97%)
  between operations  0.8 us (2%)
    pallas_call x1, Pallas kernels, per_device(): pl.pallas_call(functools.partial(first_kernel, count, step_tiles), in_spe...  23.5 us
    pallas_call x1, Pallas kernels, per_device(): pl.pallas_call(functools.partial(last_kernel, steps), grid=(steps,), in_s...  9.45 us

profile of v4, /device:TPU:16, one launch (start us, length us, event | category | flops | bytes accessed | tf_op | source)
XLA Modules:
  0.0 33.8 jit_solution(10127503225015133912)
XLA Ops:
  0.6 23.5 %softmax_and_gradient.1 = (bf16[16384,128]{1,0:T(8,128)(2,1)}, bf16[32,128,128]{2,1,0:T(8,128)(2,1)}, f32[128,128]{1,0:T(8,128)}, f32[32,512]{1,0:T(8,128)}) custom-call(bf16[16384,128]{1,0:T(8,128)(2,1)} %bitcast.3, bf16[16384,128]{1,0:T(8,128)(2,1)} %bitcast.4, bf16[4096,128]{1,0:T(8,128)(2,1)} %k_next_ref.1, bf16[4096,128]{1,0:T(8,128)(2,1)} %v_hbm.1, ...), custom_call_target="tpu_custom_call" | custom-call | tf_op jit(solution)/shard_map/softmax_and_gradient/pallas_call | solution.py:467
  24.2 9.4 %linear.1 = (bf16[4096,4,128]{2,1,0:T(4,128)(2,1)}, bf16[16384,128]{1,0:T(8,128)(2,1)}, f32[32,4,128]{2,1,0:T(4,128)}) custom-call(bf16[4096,4,128]{2,1,0:T(4,128)(2,1)} %q_ref.1, bf16[4096,128]{1,0:T(8,128)(2,1)} %k_next_ref.1, bf16[4096,128]{1,0:T(8,128)(2,1)} %k_next_ref.1, bf16[32,128,128]{2,1,0:T(8,128)(2,1)} %get-tuple-element.10.vt_ref, ...), custom_call_target="tpu_custom_call" | custom-call | tf_op jit(solution)/shard_map/linear/pallas_call | solution.py:499

commit v5 on v4

--- a/solution.py
+++ b/solution.py
@@ -337,10 +337,6 @@
         @pl.when(rank + k < count)
         def _():
             sum_copy(k).start()
-    @pl.when(rank + 1 < count)
-    def _():
-        halo_copy(0).start()
-        halo_copy(1).start()
 
     loads[3].wait()
     softmax(half + lead, blocks - half - lead)
@@ -353,6 +349,10 @@
         def _():
             sum_copy(k).wait_recv()
             state[...] += sums[k - 1].astype(F32)
+    @pl.when(rank + 1 < count)
+    def _():
+        halo_copy(0).start()
+        halo_copy(1).start()
     prefix_ref[...] = state[...].T
     loads[4].wait()
     loads[5].wait()
@@ -370,6 +370,8 @@
     for k in range(1, count):
         piece_copy(k).start()
 
+    softmax(MIDS, half - MIDS)
+
     @pl.when(rank + 1 < count)
     def _():
         halo_copy(0).wait_send()
@@ -385,7 +387,7 @@
     def _():
         k_ext[:W] = jnp.broadcast_to(k_ext[W : W + 1, :], (W, hd))
         v_ext[:MIDS] = jnp.zeros((MIDS,) + v_ext.shape[1:], BF16)
-    softmax(0, half, jnp.where(rank == 0, jnp.zeros((ONES, TILE), F32), 1.0).astype(BF16))
+    softmax(0, MIDS, jnp.where(rank == 0, jnp.zeros((ONES, TILE), F32), 1.0).astype(BF16))
 
     total = pieces[rank]
     for k in range(1, count):

time: 34 us -> 32.3 us (0.950)
  the two profiles are of different devices: /device:TPU:16 before, /device:TPU:0 now
where the time goes in v5:
time: 32.3 us; the launch traced here: 32 us
  Pallas kernels  31.2 us (97%)
  between operations  0.8 us (2%)
    pallas_call x1, Pallas kernels, per_device(): pl.pallas_call(functools.partial(first_kernel, count, step_tiles), in_spe...  21.8 us
    pallas_call x1, Pallas kernels, per_device(): pl.pallas_call(functools.partial(last_kernel, steps), grid=(steps,), in_s...  9.45 us

profile of v5, /device:TPU:0, one launch (start us, length us, event | category | flops | bytes accessed | tf_op | source)
XLA Modules:
  0.0 32.0 jit_solution(11225495442377609193)
XLA Ops:
  0.6 21.8 %softmax_and_gradient.1 = (bf16[16384,128]{1,0:T(8,128)(2,1)}, bf16[32,128,128]{2,1,0:T(8,128)(2,1)}, f32[128,128]{1,0:T(8,128)}, f32[32,512]{1,0:T(8,128)}) custom-call(bf16[16384,128]{1,0:T(8,128)(2,1)} %bitcast.3, bf16[16384,128]{1,0:T(8,128)(2,1)} %bitcast.4, bf16[4096,128]{1,0:T(8,128)(2,1)} %k_next_ref.1, bf16[4096,128]{1,0:T(8,128)(2,1)} %v_hbm.1, ...), custom_call_target="tpu_custom_call" | custom-call | tf_op jit(solution)/shard_map/softmax_and_gradient/pallas_call | solution.py:469
  22.4 9.4 %linear.1 = (bf16[4096,4,128]{2,1,0:T(4,128)(2,1)}, bf16[16384,128]{1,0:T(8,128)(2,1)}, f32[32,4,128]{2,1,0:T(4,128)}) custom-call(bf16[4096,4,128]{2,1,0:T(4,128)(2,1)} %q_ref.1, bf16[4096,128]{1,0:T(8,128)(2,1)} %k_next_ref.1, bf16[4096,128]{1,0:T(8,128)(2,1)} %k_next_ref.1, bf16[32,128,128]{2,1,0:T(8,128)(2,1)} %get-tuple-element.10.vt_ref, ...), custom_call_target="tpu_custom_call" | custom-call | tf_op jit(solution)/shard_map/linear/pallas_call | solution.py:501

commit v6 on v5

--- a/solution.py
+++ b/solution.py
@@ -94,53 +94,64 @@
     return beside([f[0] for f in found]), beside([f[1] for f in found])
 
 
-def softmax_tiles(q_ref, k_ext, v_ext, out_ref, first_tile, tiles, heads, present, meanwhile, stored):
+def softmax_parts(q_ref, k_ext, v_ext, out_ref, q_tile, first_tile, heads, sides):
     hd = q_ref.shape[1]
     rows = TILE * heads
     lanes = min(2 * TILE, rows)
     span = lanes // heads
-
     chunks = rows // lanes
-    units = tiles * chunks
     values = {}
+
+    def place(tile, i):
+        return pl.ds(pl.multiple_of(tile * rows + i * lanes, lanes), lanes)
 
     def scores(u):
         t, i = divmod(u, chunks)
-        if t >= tiles:
-            return None
         keys = k_ext[pl.ds(pl.multiple_of((first_tile + t) * TILE + i * span, span), W + span), :]
-        queries = q_ref[pl.ds(pl.multiple_of((first_tile + t) * rows + i * lanes, lanes), lanes), :]
-        return nt(keys, queries)
+        return nt(keys, q_ref[place(q_tile + t, i), :])
+
+    def weights(u, found):
+        return softmax_weights(found, u % chunks, heads, hd)
 
     def output(u, found):
         t, i = divmod(u, chunks)
         weights, total = found
         if i == 0:
             values[t] = beside([v_ext[first_tile + t + j] for j in range(MIDS + 1)])
-            if present is not None and t < MIDS:
-                ones = jnp.ones((ONES, TILE), BF16)
-                sides = [present if t + j < MIDS else ones for j in range(MIDS + 1)]
+            if sides is not None:
                 values[t] = below([values[t], beside(sides)])
         out = nn(values[t], weights)
-        if present is not None and t < MIDS:
+        if sides is not None:
             total = out[hd : hd + 1]
-        out = (out[:hd] * (1.0 / total)).astype(BF16).T
-        out_ref[pl.ds(pl.multiple_of((first_tile + t) * rows + i * lanes, lanes), lanes), :] = out
-        if i == chunks - 1:
-            stored(t)
-
+        out_ref[place(first_tile + t, i), :] = (out[:hd] * (1.0 / total)).astype(BF16).T
+
+    return chunks, scores, weights, output
+
+
+def softmax_tiles(q_ref, k_ext, v_ext, out_ref, first_tile, tiles, heads, meanwhile, stored):
+    chunks, scores, weights, output = softmax_parts(
+        q_ref, k_ext, v_ext, out_ref, first_tile, first_tile, heads, None
+    )
+    units = tiles * chunks
     ahead, behind = DEPTH * chunks, LATE * chunks
+
+    def finish(u):
+        output(u, found.pop(u))
+        if (u + 1) % chunks == 0:
+            stored(u // chunks)
+
     now = {u: scores(u) for u in range(ahead)}
     if meanwhile is not None:
         meanwhile()
     found = {}
     for u in range(units):
-        now[u + ahead] = scores(u + ahead)
-        found[u] = softmax_weights(now.pop(u), u % chunks, heads, hd)
+        if u + ahead < units:
+            now[u + ahead] = scores(u + ahead)
+        found[u] = weights(u, now.pop(u))
         if u >= behind:
-            output(u - behind, found.pop(u - behind))
+            finish(u - behind)
     for u in range(units - behind, units):
-        output(u, found.pop(u))
+        finish(u)
 
 
 def gradient_tiles(q_ref, c_ref, v_ref, kft, state, grad, before, first_tile, tiles):
@@ -187,7 +198,7 @@
     state[...] = now
 
 
-def linear_tiles(q_ref, kf_ref, vt_ref, maps_t, state, out_ref, first_token):
+def linear_tiles(q_ref, kf_ref, vt_ref, maps_t, state, out_ref, first_token, between):
     heads, hd = q_ref.shape[1:]
     tiles = q_ref.shape[0] // TILE
     ahead = later_key(heads)
@@ -225,6 +236,7 @@
         now = load(t + LAG + 1, now)
         score(t + LAG)
         output(t)
+        between(t)
     state[...] = now
     out_ref[...] = pltpu.einshape("hta->tha", below([below([d[h] for d in done])[None] for h in range(heads)]))
 
@@ -232,7 +244,7 @@
 def first_kernel(
     count, step_tiles,
     q_hbm, c_hbm, k_hbm, v_hbm, key_map_ref,
-    soft_hbm, vt_hbm, prefix_ref, mine_ref,
+    soft_hbm, vt_hbm, prefix_ref, mine_ref, rim_ref,
     q_all, c_all, k_ext, v_all, v_ext, kft, soft_all,
     local_sum, sums, halo, state, grad, pieces, pieces16, slots,
     load_sem, store_sem, sum_send, sum_recv, halo_send, halo_recv, piece_send, piece_recv,
@@ -300,12 +312,12 @@
         part = tiles_of(i * grain, grain)
         return pltpu.make_async_copy(soft_all.at[part], soft_hbm.at[part], store_sem.at[i])
 
-    def softmax(first_tile, tiles, present=None, meanwhile=None):
+    def softmax(first_tile, tiles, meanwhile=None):
         def stored(t):
             if (t + 1) % grain == 0:
                 soft_store((first_tile + t) // grain).start()
 
-        softmax_tiles(q_all, k_ext, v_ext, soft_all, first_tile, tiles, heads, present, meanwhile, stored)
+        softmax_tiles(q_all, k_ext, v_ext, soft_all, first_tile, tiles, heads, meanwhile, stored)
 
     barrier = pltpu.get_barrier_semaphore()
     for k in range(1, count):
@@ -333,7 +345,7 @@
     vt_store.start()
 
     pl.semaphore_wait(barrier, count - 1)
-    for k in range(1, count):
+    for k in reversed(range(1, count)):
         @pl.when(rank + k < count)
         def _():
             sum_copy(k).start()
@@ -367,7 +379,7 @@
             piece = turned[p * share : (p + 1) * share]
             pieces[p, :, h * hd : (h + 1) * hd] = piece
             pieces16[p, :, h * hd : (h + 1) * hd] = piece.astype(BF16)
-    for k in range(1, count):
+    for k in reversed(range(1, count)):
         piece_copy(k).start()
 
     softmax(MIDS, half - MIDS)
@@ -380,38 +392,38 @@
     def _():
         halo_copy(0).wait_recv()
         halo_copy(1).wait_recv()
-        k_ext[:W] = halo[0]
-        for b in range(MIDS):
-            v_ext[b] = halo[1, b * TILE : (b + 1) * TILE, :].T
+        rim_ref[...] = halo[...]
     @pl.when(rank == 0)
     def _():
-        k_ext[:W] = jnp.broadcast_to(k_ext[W : W + 1, :], (W, hd))
-        v_ext[:MIDS] = jnp.zeros((MIDS,) + v_ext.shape[1:], BF16)
-    softmax(0, MIDS, jnp.where(rank == 0, jnp.zeros((ONES, TILE), F32), 1.0).astype(BF16))
+        rim_ref[0] = jnp.broadcast_to(k_ext[W : W + 1, :], (W, hd))
+        rim_ref[1] = jnp.zeros((W, hd), BF16)
 
     total = pieces[rank]
     for k in range(1, count):
         piece_copy(k).wait()
         total = total + slots[k - 1].astype(F32)
     mine_ref[...] = total
-    for i in range(blocks // grain):
+    for i in range(MIDS // grain, blocks // grain):
         soft_store(i).wait()
     vt_store.wait()
 
 
 def last_kernel(
     steps,
-    q_ref, k_first_ref, k_next_ref, vt_ref, soft_in_hbm, key_map_ref, maps_ref, prefix_ref, mine_in_ref,
+    q_ref, q_own_ref, k_first_ref, k_next_ref, vt_ref, vt_first_ref, soft_in_hbm,
+    key_map_ref, maps_ref, prefix_ref, mine_in_ref, rim_ref,
     linear_ref, soft_hbm, mine_ref,
-    kf, soft_all, maps_t, state, load_sem, store_sem,
+    kf, soft_all, k_ext, v_ext, maps_t, state, load_sem, store_sem, own_sem,
 ):
     step = pl.program_id(0)
+    rank = lax.axis_index("seq")
     heads, hd = q_ref.shape[1:]
     step_tokens = q_ref.shape[0]
-    rows = step_tokens * heads
+    rows = TILE * heads
+    passed = (soft_all.shape[0] // rows - MIDS) // steps * rows
 
     def part(i):
-        return pl.ds(pl.multiple_of(i * rows, rows), rows)
+        return pl.ds(pl.multiple_of(MIDS * rows + i * passed, rows), passed)
 
     def load(i):
         return pltpu.make_async_copy(soft_in_hbm.at[part(i)], soft_all.at[part(i)], load_sem.at[i])
@@ -419,16 +431,28 @@
     def store(i):
         return pltpu.make_async_copy(soft_all.at[part(i)], soft_hbm.at[part(i)], store_sem.at[i])
 
+    def store_own(i):
+        own = at_tile(i, rows)
+        return pltpu.make_async_copy(soft_all.at[own], soft_hbm.at[own], own_sem.at[i])
+
     @pl.when(step == 0)
     def _():
-        for i in range(steps):
-            load(i).start()
+        load(0).start()
         kf[0] = nn(k_first_ref[...], key_map_ref[...]).astype(BF16)
+        k_ext[:W] = rim_ref[0]
+        k_ext[W:] = k_first_ref[:W]
+        for b in range(MIDS):
+            v_ext[b] = rim_ref[1, b * TILE : (b + 1) * TILE, :].T
+            v_ext[MIDS + b] = vt_first_ref[b]
         for h in range(heads):
             maps_t[h] = maps_ref[h].T
             mine_ref[:, h, :] = mine_in_ref[:, h * hd : (h + 1) * hd]
         state[...] = prefix_ref[...]
 
+    @pl.when(step + 1 < steps)
+    def _():
+        load(step + 1).start()
+
     @pl.when(step >= 1)
     def _():
         load(step - 1).wait()
@@ -439,14 +463,31 @@
         load(step).wait()
         store(step).start()
 
-    first_token = (lax.axis_index("seq") * steps + step) * step_tokens
-    linear_tiles(q_ref, kf.at[lax.rem(step, 2)], vt_ref, maps_t, state, linear_ref, first_token)
+    sides = [
+        jnp.where((rank == 0) & (step + j < MIDS), jnp.zeros((ONES, TILE), F32), 1.0).astype(BF16)
+        for j in range(MIDS + 1)
+    ]
+    chunks, scores, weights, output = softmax_parts(
+        q_own_ref, k_ext, v_ext, soft_all, 0, step, heads, sides
+    )
+    found = [weights(u, s) for u, s in enumerate([scores(u) for u in range(chunks)])]
+
+    def between(t):
+        if t % 2 == 0 and t // 2 < chunks:
+            output(t // 2, found[t // 2])
+
+    first_token = (rank * steps + step) * step_tokens
+    linear_tiles(
+        q_ref, kf.at[lax.rem(step, 2)], vt_ref, maps_t, state, linear_ref, first_token, between
+    )
     kf[lax.rem(step + 1, 2)] = nn(k_next_ref[...], key_map_ref[...]).astype(BF16)
+    store_own(step).start()
 
     @pl.when(step == steps - 1)
     def _():
         for i in range(steps):
             store(i).wait()
+            store_own(i).wait()
 
 
 def per_device(queries, keys, values, query_maps, key_map, linear_cotangent):
@@ -466,11 +507,11 @@
     vt16 = jax.ShapeDtypeStruct((blocks, hd, TILE), BF16)
     square = jax.ShapeDtypeStruct((hd, hd), F32)
     piece = jax.ShapeDtypeStruct((share, heads * hd), F32)
-    soft, values_t, prefix, mine = pl.pallas_call(
+    soft, values_t, prefix, mine, rim = pl.pallas_call(
         functools.partial(first_kernel, count, step_tiles),
         in_specs=[hbm, hbm, hbm, hbm, vmem],
-        out_specs=[hbm, hbm, vmem, vmem],
-        out_shape=[rows16, vt16, square, piece],
+        out_specs=[hbm, hbm, vmem, vmem, vmem],
+        out_shape=[rows16, vt16, square, piece, jax.ShapeDtypeStruct((2, W, hd), BF16)],
         scratch_shapes=[
             pltpu.VMEM(flat, BF16),
             pltpu.VMEM(flat, BF16),
@@ -503,23 +544,30 @@
         grid=(steps,),
         in_specs=[
             along,
+            pl.BlockSpec((TILE * heads, hd), lambda i: (i, 0)),
             pl.BlockSpec((tokens, hd), lambda i: (0, 0), pipeline_mode=pl.Buffered(1)),
             pl.BlockSpec((tokens, hd), lambda i: (jnp.minimum(i + 1, steps - 1), 0)),
             pl.BlockSpec((step_tiles, hd, TILE), lambda i: (i, 0, 0)),
-            hbm, once(key_map), once(query_maps), once(prefix), once(mine),
+            pl.BlockSpec((MIDS, hd, TILE), lambda i: (0, 0, 0), pipeline_mode=pl.Buffered(1)),
+            hbm, once(key_map), once(query_maps), once(prefix), once(mine), once(rim),
         ],
         out_specs=[along, hbm, once(final)],
         out_shape=[jax.ShapeDtypeStruct((tokens_here, heads, hd), BF16), rows16, final],
         scratch_shapes=[
             pltpu.VMEM((2, tokens, hd), BF16),
             pltpu.VMEM(flat, BF16),
+            pltpu.VMEM((2 * W, hd), BF16),
+            pltpu.VMEM((2 * MIDS, hd, TILE), BF16),
             pltpu.VMEM((heads, hd, hd), BF16),
             pltpu.VMEM((hd, hd), F32),
-            dma((steps,)), dma((steps,)),
+            dma((steps,)), dma((steps,)), dma((steps,)),
         ],
         compiler_params=pltpu.CompilerParams(dimension_semantics=("arbitrary",)),
         name="linear",
-    )(queries, keys, keys, values_t, soft, key_map, query_maps, prefix, mine)
+    )(
+        queries, queries.reshape(flat), keys, keys, values_t, values_t, soft,
+        key_map, query_maps, prefix, mine, rim,
+    )
     return soft.reshape(queries.shape), linear, mine
 
 

time: 32.3 us -> 35 us (1.084)
  Pallas kernels: 31.2 us -> 33.9 us
    pallas_call x1, Pallas kernels: 9.45 us -> 11.3 us  [per_device(): pl.pallas_call(functools.partial(last_kernel, steps), grid=(steps,), in_s...]
    pallas_call x1, Pallas kernels: 21.8 us -> 22.6 us  [per_device(): pl.pallas_call(functools.partial(first_kernel, count, step_tiles), in_spe...]
where the time goes in v6:
time: 35 us; the launch traced here: 34.7 us
  Pallas kernels  33.9 us (97%)
  between operations  0.8 us (2%)
    pallas_call x1, Pallas kernels, per_device(): pl.pallas_call(functools.partial(first_kernel, count, step_tiles), in_spe...  22.6 us
    pallas_call x1, Pallas kernels, per_device(): pl.pallas_call(functools.partial(last_kernel, steps), grid=(steps,), in_s...  11.3 us

profile of v6, /device:TPU:0, one launch (start us, length us, event | category | flops | bytes accessed | tf_op | source)
XLA Modules:
  0.0 34.7 jit_solution(14513055394094705877)
XLA Ops:
  0.6 22.6 %softmax_and_gradient.1 = (bf16[16384,128]{1,0:T(8,128)(2,1)}, bf16[32,128,128]{2,1,0:T(8,128)(2,1)}, f32[128,128]{1,0:T(8,128)}, f32[32,512]{1,0:T(8,128)}, bf16[2,512,128]{2,1,0:T(8,128)(2,1)}) custom-call(bf16[16384,128]{1,0:T(8,128)(2,1)} %bitcast.3, bf16[16384,128]{1,0:T(8,128)(2,1)} %bitcast.5, bf16[4096,128]{1,0:T(8,128)(2,1)} %k_next_ref.1, ...), custom_call_target="tpu_custom_call" | custom-call | tf_op jit(solution)/shard_map/softmax_and_gradient/pallas_call | solution.py:510
  23.3 11.3 %linear.1 = (bf16[4096,4,128]{2,1,0:T(4,128)(2,1)}, bf16[16384,128]{1,0:T(8,128)(2,1)}, f32[32,4,128]{2,1,0:T(4,128)}) custom-call(bf16[4096,4,128]{2,1,0:T(4,128)(2,1)} %q_ref.1, bf16[16384,128]{1,0:T(8,128)(2,1)} %bitcast.4, bf16[4096,128]{1,0:T(8,128)(2,1)} %k_next_ref.1, bf16[4096,128]{1,0:T(8,128)(2,1)} %k_next_ref.1, ...), custom_call_target="tpu_custom_call" | custom-call | tf_op jit(solution)/shard_map/linear/pallas_call | solution.py:542

commit v7 on v5

--- a/solution.py
+++ b/solution.py
@@ -333,7 +333,7 @@
     vt_store.start()
 
     pl.semaphore_wait(barrier, count - 1)
-    for k in range(1, count):
+    for k in reversed(range(1, count)):
         @pl.when(rank + k < count)
         def _():
             sum_copy(k).start()
@@ -367,7 +367,7 @@
             piece = turned[p * share : (p + 1) * share]
             pieces[p, :, h * hd : (h + 1) * hd] = piece
             pieces16[p, :, h * hd : (h + 1) * hd] = piece.astype(BF16)
-    for k in range(1, count):
+    for k in reversed(range(1, count)):
         piece_copy(k).start()
 
     softmax(MIDS, half - MIDS)

time: 32.3 us -> 33 us (1.022)
  Pallas kernels: 31.2 us -> 31.9 us
    pallas_call x1, Pallas kernels: 21.8 us -> 22.5 us  [per_device(): pl.pallas_call(functools.partial(first_kernel, count, step_tiles), in_spe...]
where the time goes in v7:
time: 33 us; the launch traced here: 32.7 us
  Pallas kernels  31.9 us (97%)
  between operations  0.8 us (2%)
    pallas_call x1, Pallas kernels, per_device(): pl.pallas_call(functools.partial(first_kernel, count, step_tiles), in_spe...  22.5 us
    pallas_call x1, Pallas kernels, per_device(): pl.pallas_call(functools.partial(last_kernel, steps), grid=(steps,), in_s...  9.45 us

profile of v7, /device:TPU:0, one launch (start us, length us, event | category | flops | bytes accessed | tf_op | source)
XLA Modules:
  0.0 32.7 jit_solution(3864869809105305004)
XLA Ops:
  0.6 22.5 %softmax_and_gradient.1 = (bf16[16384,128]{1,0:T(8,128)(2,1)}, bf16[32,128,128]{2,1,0:T(8,128)(2,1)}, f32[128,128]{1,0:T(8,128)}, f32[32,512]{1,0:T(8,128)}) custom-call(bf16[16384,128]{1,0:T(8,128)(2,1)} %bitcast.3, bf16[16384,128]{1,0:T(8,128)(2,1)} %bitcast.4, bf16[4096,128]{1,0:T(8,128)(2,1)} %k_next_ref.1, bf16[4096,128]{1,0:T(8,128)(2,1)} %v_hbm.1, ...), custom_call_target="tpu_custom_call" | custom-call | tf_op jit(solution)/shard_map/softmax_and_gradient/pallas_call | solution.py:469
  23.1 9.5 %linear.1 = (bf16[4096,4,128]{2,1,0:T(4,128)(2,1)}, bf16[16384,128]{1,0:T(8,128)(2,1)}, f32[32,4,128]{2,1,0:T(4,128)}) custom-call(bf16[4096,4,128]{2,1,0:T(4,128)(2,1)} %q_ref.1, bf16[4096,128]{1,0:T(8,128)(2,1)} %k_next_ref.1, bf16[4096,128]{1,0:T(8,128)(2,1)} %k_next_ref.1, bf16[32,128,128]{2,1,0:T(8,128)(2,1)} %get-tuple-element.10.vt_ref, ...), custom_call_target="tpu_custom_call" | custom-call | tf_op jit(solution)/shard_map/linear/pallas_call | solution.py:501

commit v8 on v7

--- a/solution.py
+++ b/solution.py
@@ -242,7 +242,7 @@
     tokens_here = v_all.shape[0]
     blocks = tokens_here // TILE
     share = hd // count
-    half = blocks // 2
+    half = blocks // 2 + 2
     before = rank * tokens_here
 
     def halo_copy(i):
@@ -277,7 +277,7 @@
         )
 
     rows = TILE * heads
-    lead = 3 * step_tiles // 4
+    lead = step_tiles // 2
     grain = 2
 
     def tiles_of(first, tiles):
@@ -367,7 +367,7 @@
             piece = turned[p * share : (p + 1) * share]
             pieces[p, :, h * hd : (h + 1) * hd] = piece
             pieces16[p, :, h * hd : (h + 1) * hd] = piece.astype(BF16)
-    for k in reversed(range(1, count)):
+    for k in range(1, count):
         piece_copy(k).start()
 
     softmax(MIDS, half - MIDS)

time: 33 us -> 32.9 us (level)
  no operation moved by 1% of the time
where the time goes in v8:
time: 32.9 us; the launch traced here: 32.7 us
  Pallas kernels  31.9 us (97%)
  between operations  0.8 us (2%)
    pallas_call x1, Pallas kernels, per_device(): pl.pallas_call(functools.partial(first_kernel, count, step_tiles), in_spe...  22.5 us
    pallas_call x1, Pallas kernels, per_device(): pl.pallas_call(functools.partial(last_kernel, steps), grid=(steps,), in_s...  9.45 us

profile of v8, /device:TPU:0, one launch (start us, length us, event | category | flops | bytes accessed | tf_op | source)
XLA Modules:
  0.0 32.7 jit_solution(10331483057528261766)
XLA Ops:
  0.6 22.5 %softmax_and_gradient.1 = (bf16[16384,128]{1,0:T(8,128)(2,1)}, bf16[32,128,128]{2,1,0:T(8,128)(2,1)}, f32[128,128]{1,0:T(8,128)}, f32[32,512]{1,0:T(8,128)}) custom-call(bf16[16384,128]{1,0:T(8,128)(2,1)} %bitcast.3, bf16[16384,128]{1,0:T(8,128)(2,1)} %bitcast.4, bf16[4096,128]{1,0:T(8,128)(2,1)} %k_next_ref.1, bf16[4096,128]{1,0:T(8,128)(2,1)} %v_hbm.1, ...), custom_call_target="tpu_custom_call" | custom-call | tf_op jit(solution)/shard_map/softmax_and_gradient/pallas_call | solution.py:469
  23.1 9.4 %linear.1 = (bf16[4096,4,128]{2,1,0:T(4,128)(2,1)}, bf16[16384,128]{1,0:T(8,128)(2,1)}, f32[32,4,128]{2,1,0:T(4,128)}) custom-call(bf16[4096,4,128]{2,1,0:T(4,128)(2,1)} %q_ref.1, bf16[4096,128]{1,0:T(8,128)(2,1)} %k_next_ref.1, bf16[4096,128]{1,0:T(8,128)(2,1)} %k_next_ref.1, bf16[32,128,128]{2,1,0:T(8,128)(2,1)} %get-tuple-element.10.vt_ref, ...), custom_call_target="tpu_custom_call" | custom-call | tf_op jit(solution)/shard_map/linear/pallas_call | solution.py:501
